TPU v7x, 32 devices: a whole 2x2x4 slice. The times are simulated.
32 devices in a mesh: parts: 2 (over y), tm: 4 (over z), head: 2 (over x), sub: 2 (over core).
Axes of the slice: x: 2, y: 2, z: 4, core: 2. Of those that a mesh axis runs over, the one named last changes fastest.
Arguments:
- signal: bfloat16 [32768, 2048], P(('parts', 'tm'), ('head', 'sub')), parts along dimension 0, may hold values from -6 to 6
- entry_map: bfloat16 [32768, 128], P(('parts', 'tm')), parts along dimension 0, may hold values from -6 to 6
- readout: bfloat16 [32768, 128], P(('parts', 'tm')), parts along dimension 0, may hold values from -6 to 6
- gate_input: bfloat16 [32768, 2048], P(('parts', 'tm'), ('head', 'sub')), parts along dimension 0, may hold values from -40 to 40
- log_decay: float32 [32, 32768], P(('head', 'sub'), ('parts', 'tm')), parts along dimension 1, may hold values from -0.6 to 0, as said below
- norm_gain: float32 [2048], P(('head', 'sub')), may hold values from 0.5 to 1.5
Outputs:
- layer_out: bfloat16 [32768, 2048], P(('parts', 'tm'), ('head', 'sub')), parts along dimension 0
There are 2 independent parts, one for each index of `parts`. A program takes and returns all parts, laid end to end along the dimension named above; an argument that names none is the same for every part. Nothing has to cross between parts.
Inputs may be any that keep to these rules, and one draw needn't show every extreme that they name: `log_decay`: never positive.
All inputs are finite; a program needn't handle non-finite values.
Results may differ from a plain program's by a relative error of at most 0.0075.
Values sent between devices are 32-bit elements; how exact they have to be, the bound alone decides.
No kernel may reach another device: no remote copies, remote signals or barrier semaphores. Data moves between devices by JAX's collectives and lax.ppermute only.
A program may use at most 128 MiB of HBM per device.

v0:
```python
import jax
import jax.numpy as jnp
from jax import lax
from jax.sharding import PartitionSpec as P

SPAN = 256


epsilon = 1e-05


def carry_matrix(prior_value, through):
    number = prior_value.shape[0]
    strict = jnp.tril(jnp.ones((number, number), bool), -1)
    spread = prior_value.T[:, :, None] - through.T[:, None, :]
    return jnp.where(strict, jnp.exp(jnp.where(strict, spread, 0.0)), 0.0)


def shards(signal, entry_map, readout, gate_input, log_decay, norm_gain):
    head_count = log_decay.shape[0]
    length = signal.shape[0]
    head_size = signal.shape[1] // head_count
    state_size = entry_map.shape[1]
    blocks = length // SPAN
    signals = signal.reshape(blocks, SPAN, head_count, head_size)
    entries = entry_map.reshape(blocks, SPAN, state_size)
    readouts = readout.reshape(blocks, SPAN, state_size)
    running = jnp.cumsum(log_decay.reshape(head_count, blocks, SPAN).transpose(1, 0, 2), axis=2)
    scores = jnp.einsum("ctn,csn->cts", readouts, entries, preferred_element_type=jnp.float32)
    causal = jnp.tril(jnp.ones((SPAN, SPAN), bool))
    spread = running[:, :, :, None] - running[:, :, None, :]
    decays = jnp.where(causal, jnp.exp(jnp.where(causal, spread, 0.0)), 0.0)
    weights = (scores[:, None] * decays).astype(jnp.bfloat16)
    inside = jnp.einsum("chts,cshp->cthp", weights, signals, preferred_element_type=jnp.float32)
    remains = jnp.exp(running[:, :, -1:] - running)
    written = (entries[:, None].astype(jnp.float32) * remains[..., None]).astype(jnp.bfloat16)
    states = jnp.einsum("cshp,chsn->chpn", signals, written, preferred_element_type=jnp.float32)
    totals = running[:, :, -1]
    all_totals = lax.all_gather(totals, "tm", axis=0, tiled=True)
    through = jnp.cumsum(all_totals, axis=0)
    matrix = carry_matrix(through - all_totals, through)
    pieces = lax.all_to_all(states, "tm", split_axis=2, concat_axis=0, tiled=True)
    blended = jnp.einsum(
        "hcd,dhpn->chpn",
        matrix,
        pieces,
        precision=lax.Precision.HIGHEST,
        preferred_element_type=jnp.float32,
    )
    incoming = lax.all_to_all(blended, "tm", split_axis=0, concat_axis=2, tiled=True)
    upper_part = incoming.astype(jnp.bfloat16)
    lower_part = (incoming - upper_part.astype(jnp.float32)).astype(jnp.bfloat16)
    across = jnp.einsum("ctn,chpn->cthp", readouts, upper_part, preferred_element_type=jnp.float32)
    across = across + jnp.einsum(
        "ctn,chpn->cthp", readouts, lower_part, preferred_element_type=jnp.float32
    )
    across = across * jnp.exp(running).transpose(0, 2, 1)[..., None]
    output = (inside + across).reshape(length, head_count, head_size)
    gated_out = output * jax.nn.silu(
        gate_input.reshape(length, head_count, head_size).astype(jnp.float32)
    )
    scaled = gated_out * lax.rsqrt(
        jnp.mean(gated_out * gated_out, axis=-1, keepdims=True) + epsilon
    )
    scaled = scaled * norm_gain.reshape(head_count, head_size)
    return scaled.reshape(length, head_count * head_size).astype(jnp.bfloat16)


def solution(mesh):
    in_specs = (
        P(("parts", "tm"), ("head", "sub")),
        P(("parts", "tm"), None),
        P(("parts", "tm"), None),
        P(("parts", "tm"), ("head", "sub")),
        P(("head", "sub"), ("parts", "tm")),
        P(("head", "sub")),
    )
    out_specs = P(("parts", "tm"), ("head", "sub"))
    return jax.shard_map(shards, mesh=mesh, in_specs=in_specs, out_specs=out_specs, check_vma=False)
```

profile of v0, /device:TPU:0, one launch (start us, length us, event | category | flops | bytes accessed | tf_op | source)
XLA Modules:
  0.0 313.1 jit_solution(16196469978576982656)
XLA Ops:
  0.0 15.8 %reduce-window.6 = f32[16,8,2,128]{3,1,2,0:T(8,128)S(1)} reduce-window(f32[16,8,2,128]{3,1,2,0:T(8,128)} %bitcast.94, f32[]{:T(128)} %constant.12.clone.1), window={size=1x1x1x128 pad=0_0x0_0x0_0x127_0}, to_apply=%region_0.0 | reduce-window | flops 4161536 | bytes 262148 | tf_op jit(solution)/shard_map/reduce-window
  16.7 1.4 convert_element_type.37
  18.1 11.2 %reshape.106 = bf16[16,256,8,64]{3,2,1,0:T(8,128)(2,1)} reshape(bf16[4096,512]{1,0:T(8,128)(2,1)} %param.6) | data formatting | bytes 8388608 | tf_op jit(solution)/shard_map/reshape | solution.py:25
  29.3 9.1 %copy.39 = bf16[16,256,8,64]{1,3,2,0:T(8,128)(2,1)} copy(bf16[16,256,8,64]{3,2,1,0:T(8,128)(2,1)} %reshape.106) | data formatting | bytes 8388608 | tf_op jit(solution)/shard_map/reshape | solution.py:25
  38.4 8.3 %fusion.13 = f32[16,8,64,128]{3,2,1,0:T(8,128)S(1)} fusion(bf16[16,256,8,64]{1,3,2,0:T(8,128)(2,1)} %copy.39, f32[16,8,256]{2,1,0:T(8,128)S(1)} %subtract_exponential_fusion, f32[16,256,128]{2,1,0:T(8,128)S(1)} %convert_element_type.37), kind=kOutput, calls=%fused_computation.20 | convolution fusion | flops 545259520 | bytes 10616832 | tf_op jit(solution)/shard_map/cshp,chsn->chpn/dot_general | solution.py:37
  46.7 4.4 %copy.44 = f32[16,8,64,128]{3,1,0,2:T(8,128)} copy(f32[16,8,64,128]{3,2,1,0:T(8,128)S(1)} %fusion.13) | data formatting | bytes 8388608 | tf_op jit(solution)/shard_map/cshp,chsn->chpn/dot_general | solution.py:37
  51.2 6.3 %all-to-all-start = ((f32[16,8,64,128]{3,1,0,2:T(8,128)}), f32[16,8,64,128]{3,1,0,2:T(8,128)}, u32[]{:S(2)}, u32[]{:S(2)}) async-start(f32[16,8,64,128]{3,1,0,2:T(8,128)} %copy.44), calls=%async_computation | async-start | bytes 8388608 | tf_op jit(solution)/shard_map/all_to_all | solution.py:42
  57.5 98.7 %all-gather = f32[64,8,1]{1,0,2:T(8,128)S(1)} all-gather(f32[16,8,1]{1,0,2:T(8,128)S(1)} %copy.60), channel_id=2, replica_groups=mesh['parts'=2,'tm'=4,'head'=2,'sub'=2] {'tm'}, dimensions={0}, use_global_device_ids=true | all-gather | bytes 2560 | tf_op jit(solution)/shard_map/all_gather | solution.py:39
  156.6 3.0 copy.45
  159.6 4.1 %convolution_bitcast_fusion = f32[64,8,16,128]{3,0,2,1:T(8,128)S(1)} fusion(f32[64,8,16,128]{3,0,2,1:T(8,128)S(1)} %bitcast.85, f32[8,64]{1,0:T(8,128)S(1)} %copy.47, f32[8,64]{1,0:T(8,128)S(1)} %copy.46, pred[64,64]{1,0:T(8,128)(4,1)S(1)} %iota_compare_fusion.1), kind=kOutput, calls=%fused_computation.21 | convolution fusion | flops 805404672 | bytes 8396800 | tf_op jit(solution)/shard_map/hcd,dhpn->chpn/dot_general | solution.py:43
  163.6 4.4 %copy.48 = f32[64,8,16,128]{3,2,1,0:T(8,128)} copy(f32[64,8,16,128]{3,0,2,1:T(8,128)S(1)} %convolution_bitcast_fusion) | data formatting | bytes 8388608 | tf_op jit(solution)/shard_map/hcd,dhpn->chpn/transpose | solution.py:43
  168.0 5.0 %all-to-all-start.1 = ((f32[64,8,16,128]{3,2,1,0:T(8,128)}), f32[64,8,16,128]{3,2,1,0:T(8,128)}, u32[]{:S(2)}, u32[]{:S(2)}) async-start(f32[64,8,16,128]{3,2,1,0:T(8,128)} %copy.48), calls=%async_computation.1 | async-start | bytes 8388608 | tf_op jit(solution)/shard_map/all_to_all | solution.py:50
  173.1 6.3 %copy.51 = bf16[4096,512]{0,1:T(8,128)(2,1)} copy(bf16[4096,512]{1,0:T(8,128)(2,1)} %param.9) | data formatting | bytes 8388608 | tf_op args[3]
  179.4 3.3 %convert_element_type.42 = f32[4096,512]{0,1:T(8,128)S(1)} convert(bf16[4096,512]{0,1:T(8,128)(2,1)} %copy.51) | non-fusion elementwise | flops 2097152 | bytes 12582912 | tf_op jit(solution)/shard_map/convert_element_type | solution.py:60
  182.7 7.2 %copy.62 = f32[64,8,16,256]{3,2,1,0:T(8,128)} copy(f32[64,8,16,256]{3,1,2,0:T(8,128)S(1)} %bitcast.84) | data formatting | bytes 16777216
  190.7 11.0 %fusion = f32[16,8,256,64]{2,3,1,0:T(8,128)} fusion(bf16[16,256,8,64]{1,3,2,0:T(8,128)(2,1)S(1)} %copy-done.2, f32[16,8,256]{2,1,0:T(8,128)S(1)} %get-tuple-element.8, f32[16,256,256]{2,1,0:T(8,128)S(1)} %fusion.27, pred[256,256]{1,0:T(8,128)(4,1)S(1)} %iota_compare_fusion), kind=kOutput, calls=%fused_computation.1 | convolution fusion | flops 1115684864 | bytes 16973824 | tf_op jit(solution)/shard_map/chts,cshp->cthp/dot_general | solution.py:34
  201.7 62.2 %all-to-all-done.1 = f32[64,8,16,128]{3,2,1,0:T(8,128)} async-done(((f32[64,8,16,128]{3,2,1,0:T(8,128)}), f32[64,8,16,128]{3,2,1,0:T(8,128)}, u32[]{:S(2)}, u32[]{:S(2)}) %all-to-all-start.1) | async-done | bytes 4194336 | tf_op jit(solution)/shard_map/all_to_all | solution.py:50
  263.9 2.7 copy.49
  267.3 4.6 %fusion.28 = f32[16,8,64,256]{3,2,1,0:T(8,128)} fusion(bf16[16,8,64,128]{3,2,1,0:T(8,128)(2,1)S(1)} %get-tuple-element.6, bf16[16,256,128,1]{2,1,3,0:T(8,128)(2,1)S(1)} %bitcast.79), kind=kOutput, calls=%fused_computation.44 | convolution fusion | flops 536870912 | bytes 11534336 | tf_op jit(solution)/shard_map/ctn,chpn->cthp/dot_general | solution.py:53
  271.9 12.6 %multiply_reduce_fusion = (f32[16,256,8]{1,2,0:T(8,128)S(1)}, f32[16,256,8,64]{1,3,2,0:T(8,128)}) fusion(f32[16,256,8,64]{1,0,3,2:T(8,128)S(1)} %bitcast.88, f32[16,256,8]{1,2,0:T(8,128)S(1)} %get-tuple-element.7, f32[16,8,64,256]{3,2,1,0:T(8,128)} %fusion.28, bf16[16,8,64,128]{3,2,1,0:T(8,128)(2,1)S(1)} %get-tuple-element.5, ...), kind=kOutput, calls=%fused_computation.14 | convolution fusion | flops 557809664 | bytes 36962304 | tf_op jit(solution)/shard_map/ctn,chpn->cthp/dot_general | solution.py:54
  284.6 8.1 %copy.50 = f32[16,256,8,64]{1,0,3,2:T(8,128)S(1)} copy(f32[16,256,8,64]{1,3,2,0:T(8,128)} %get-tuple-element.10) | data formatting | bytes 16777216 | tf_op jit(solution)/shard_map/add | solution.py:58
  292.7 8.5 %copy.61 = f32[64,8,16,256]{3,1,2,0:T(8,128)S(1)} copy(f32[64,8,16,256]{3,2,1,0:T(8,128)S(1)} %bitcast.83) | data formatting | bytes 16777216
  301.2 5.0 %fusion.8 = bf16[4096,512]{0,1:T(8,128)(2,1)} fusion(f32[4096,512]{0,1:T(8,128)S(1)} %bitcast.82, f32[512]{0:T(512)S(1)} %copy-done.4, f32[4096,8]{0,1:T(8,128)S(1)} %bitcast.91, bf16[4096,512]{0,1:T(8,128)(2,1)S(1)} %copy-done.1), kind=kLoop, calls=%fused_computation.11 | loop fusion | flops 18874368 | bytes 16910336 | tf_op jit(solution)/shard_map/convert_element_type | solution.py:66
  306.2 6.4 %copy.54 = bf16[4096,512]{1,0:T(8,128)(2,1)} copy(bf16[4096,512]{0,1:T(8,128)(2,1)} %fusion.8) | data formatting | bytes 8388608 | tf_op jit(solution)/shard_map/convert_element_type | solution.py:66
  (35 shorter events, 2.6 us)
Async XLA Ops:
  0.0 189.9 %copy-start = (bf16[4096,128]{1,0:T(8,128)(2,1)S(1)}, bf16[4096,128]{1,0:T(8,128)(2,1)}, u32[]{:S(2)}) copy-start(bf16[4096,128]{1,0:T(8,128)(2,1)} %param.8) | copy-start | bytes 3145732
  51.2 105.4 %all-to-all-start = ((f32[16,8,64,128]{3,1,0,2:T(8,128)}), f32[16,8,64,128]{3,1,0,2:T(8,128)}, u32[]{:S(2)}, u32[]{:S(2)}) async-start(f32[16,8,64,128]{3,1,0,2:T(8,128)} %copy.44), calls=%async_computation | async-start | bytes 8388608 | tf_op jit(solution)/shard_map/all_to_all | solution.py:42
  168.0 95.9 %all-to-all-start.1 = ((f32[64,8,16,128]{3,2,1,0:T(8,128)}), f32[64,8,16,128]{3,2,1,0:T(8,128)}, u32[]{:S(2)}, u32[]{:S(2)}) async-start(f32[64,8,16,128]{3,2,1,0:T(8,128)} %copy.48), calls=%async_computation.1 | async-start | bytes 8388608 | tf_op jit(solution)/shard_map/all_to_all | solution.py:50
  182.7 7.3 %copy-start.3 = (bf16[4096,128]{1,0:T(8,128)(2,1)S(1)}, bf16[4096,128]{1,0:T(8,128)(2,1)}, u32[]{:S(2)}) copy-start(bf16[4096,128]{1,0:T(8,128)(2,1)} %param.7) | copy-start | bytes 3145732
  182.7 8.0 %copy-start.2 = (bf16[16,256,8,64]{1,3,2,0:T(8,128)(2,1)S(1)}, bf16[16,256,8,64]{1,3,2,0:T(8,128)(2,1)}, u32[]{:S(2)}) copy-start(bf16[16,256,8,64]{1,3,2,0:T(8,128)(2,1)} %copy.39) | copy-start | bytes 12582916
  266.6 5.3 %slice-start = ((s8[8388608]{0:T(1024)(128)(4,1)}), s8[4194304]{0:T(1024)(128)(4,1)S(1)}, s32[]{:S(2)}) async-start(s8[8388608]{0:T(1024)(128)(4,1)} %bitcast.86), calls=%async_computation.2 | async-start | bytes 8388608
  267.3 4.6 %slice-start.1 = ((s8[8388608]{0:T(1024)(128)(4,1)}), s8[4194304]{0:T(1024)(128)(4,1)S(1)}, s32[]{:S(2)}) async-start(s8[8388608]{0:T(1024)(128)(4,1)} %bitcast.86), calls=%async_computation.3 | async-start | bytes 8388608
  292.7 8.5 %copy-start.1 = (bf16[4096,512]{0,1:T(8,128)(2,1)S(1)}, bf16[4096,512]{0,1:T(8,128)(2,1)}, u32[]{:S(2)}) copy-start(bf16[4096,512]{0,1:T(8,128)(2,1)} %copy.51) | copy-start | bytes 12582916
  292.7 8.5 %copy-start.4 = (f32[512]{0:T(512)S(1)}, f32[512]{0:T(512)}, u32[]{:S(2)}) copy-start(f32[512]{0:T(512)} %param.11) | copy-start | bytes 6148
where the time goes:
time: 319 us; the launch traced here: 313 us
  blocking collectives  98.7 us (31%)
  local copies, waits for them, and re-layouts  72 us (23%)
  waiting for transfers between devices  62.2 us (19%)
  matrix products  41.4 us (13%)
  other arithmetic  26.6 us (8%)
  starting transfers between devices  11.4 us (4%)
    all_gather x1, blocking collectives, shards(): all_totals = lax.all_gather(totals, 'tm', axis=0, tiled=True)  98.7 us
    all_to_all x1, waiting for transfers between devices, shards(): lax.all_to_all(blended, 'tm', split_axis=0, concat_axis=2, tiled=True)  62.2 us
    unnamed x18, local copies, waits for them, and re-layouts  22.2 us
    reshape x2, local copies, waits for them, and re-layouts, shards(): signals = signal.reshape(blocks, SPAN, head_count, head_size)  20.3 us
    another operation x2, other arithmetic  15.8 us
    dot_general x1, matrix products, shards(): jnp.einsum('ctn,chpn->cthp', readouts, lower_part, preferred_element_type...  12.6 us
    dot_general x1, matrix products, shards(): jnp.einsum('chts,cshp->cthp', weights, signals, preferred_element_type=jn...  11 us
    dot_general x1, matrix products, shards(): jnp.einsum('cshp,chsn->chpn', signals, written, preferred_element_type=jn...  8.33 us
  transfers between devices with their start and end apart: 2, of which 1 were waited for; matrix products, arithmetic and copies ran while one was open for 9% of the time, Pallas kernels for 0%

commit v1 on v0

v1 whole, which is shorter than its diff:
```python
import functools

import jax
import jax.numpy as jnp
from jax import lax
from jax.experimental import pallas as pl
from jax.experimental.pallas import tpu as pltpu
from jax.sharding import PartitionSpec as P

CHUNK = 128
HEAD_ROWS = 8
EPSILON = 1e-05
F32 = jnp.float32
BF16 = jnp.bfloat16
TN = (((0,), (0,)), ((), ()))
NT = (((1,), (1,)), ((), ()))


def mm(left, right, dims=(((1,), (0,)), ((), ()))):
    return lax.dot_general(left, right, dims, preferred_element_type=F32)


def two_terms(value):
    high = value.astype(BF16)
    return high, (value - high.astype(F32)).astype(BF16)


def spread_matrix(width, head_size):
    row = lax.broadcasted_iota(jnp.int32, (2 * HEAD_ROWS, width), 0)
    column = lax.broadcasted_iota(jnp.int32, (2 * HEAD_ROWS, width), 1)
    own = lax.rem(row, HEAD_ROWS) == lax.div(column, head_size)
    return own.astype(F32).astype(BF16)


def stacked(decay):
    chunks = decay.shape[1] // CHUNK
    return jnp.concatenate([decay[:, c * CHUNK : (c + 1) * CHUNK] for c in range(chunks)], axis=0)


def sums(decay_rows, matrix):
    high = decay_rows.astype(BF16)
    rest = decay_rows - high.astype(F32)
    middle = rest.astype(BF16)
    low = (rest - middle.astype(F32)).astype(BF16)
    return mm(high, matrix) + (mm(middle, matrix) + mm(low, matrix))


def pair_rows(value):
    high, low = two_terms(value)
    return jnp.concatenate([high, low], axis=0)


def indicator(test):
    return test.astype(F32).astype(BF16)


def state_kernel(split, head_size, place_ref, decay_ref, entry_ref, signal_ref, *rest):
    outs, (factor_ref, total_ref, state_ref) = rest[:-3], rest[-3:]
    step = pl.program_id(0)
    rows, width = signal_ref.shape
    per_tile = rows // CHUNK
    spread = spread_matrix(width, head_size)

    @pl.when(step == 0)
    def _():
        tall = stacked(decay_ref[...])
        chunks = tall.shape[0] // HEAD_ROWS
        s_from = lax.broadcasted_iota(jnp.int32, (CHUNK, 2 * CHUNK), 0)
        s_to = lax.broadcasted_iota(jnp.int32, (CHUNK, 2 * CHUNK), 1)
        both = sums(tall, indicator((s_from > s_to) | (s_to >= CHUNK)))
        later = jnp.zeros((HEAD_ROWS, CHUNK), F32)
        for c in reversed(range(chunks)):
            part = both[c * HEAD_ROWS : (c + 1) * HEAD_ROWS]
            factor_ref[c] = pair_rows(jnp.exp(part[:, :CHUNK] + later))
            later = later + part[:, CHUNK:]
        total_ref[...] = later
        state_ref[...] = jnp.zeros_like(state_ref)

    added = None
    for start in range(0, per_tile, 2):
        many = min(2, per_tile - start)
        where = pl.ds(start * CHUNK, many * CHUNK)
        factor = jnp.concatenate(
            [mm(factor_ref[step * per_tile + start + k], spread, TN) for k in range(many)], axis=0
        )
        scaled = (signal_ref[where, :].astype(F32) * factor).astype(BF16)
        term = mm(entry_ref[where, :], scaled, TN)
        added = term if added is None else added + term
    state_ref[...] += added

    @pl.when(step == pl.num_programs(0) - 1)
    def _():
        gain = mm(pair_rows(jnp.exp(total_ref[:, :HEAD_ROWS])), spread, TN)
        states = state_ref[...]
        size = states.shape[0]
        if split:
            own_ref, first_ref, second_ref = outs
            half = width // 2
            place = place_ref[0]
            for k in range(2):
                own_ref[k, :size, :] = states[:, k * half : (k + 1) * half]
                own_ref[k, size:, :] = gain[:, k * half : (k + 1) * half]

            @pl.when(place == 0)
            def _():
                first_ref[...] = own_ref[0]
                second_ref[...] = own_ref[1]

            @pl.when(place != 0)
            def _():
                first_ref[...] = own_ref[1]
                second_ref[...] = own_ref[0]
        else:
            (own_ref,) = outs
            own_ref[:size, :] = states
            own_ref[size:, :] = gain


def local_states(place, decay, entry_map, signal, head_size, split, tile):
    length, width = signal.shape
    state_size = entry_map.shape[1]
    tall = state_size + HEAD_ROWS
    if split:
        shapes = [(2, tall, width // 2), (tall, width // 2), (tall, width // 2)]
    else:
        shapes = [(tall, width)]
    whole = [pl.BlockSpec(s, functools.partial(lambda r, i: (0,) * r, len(s))) for s in shapes]
    return pl.pallas_call(
        functools.partial(state_kernel, split, head_size),
        grid=(length // tile,),
        in_specs=[
            pl.BlockSpec(memory_space=pltpu.SMEM),
            pl.BlockSpec((HEAD_ROWS, length), lambda i: (0, 0)),
            pl.BlockSpec((tile, state_size), lambda i: (i, 0)),
            pl.BlockSpec((tile, width), lambda i: (i, 0)),
        ],
        out_specs=whole,
        out_shape=[jax.ShapeDtypeStruct(s, F32) for s in shapes],
        scratch_shapes=[
            pltpu.VMEM((length // CHUNK, 2 * HEAD_ROWS, CHUNK), BF16),
            pltpu.VMEM((HEAD_ROWS, CHUNK), F32),
            pltpu.VMEM((state_size, width), F32),
        ],
        name="device_states",
        cost_estimate=pl.CostEstimate(
            flops=2 * length * width * state_size,
            bytes_accessed=2 * length * (width + state_size),
            transcendentals=0,
        ),
    )(place, decay, entry_map, signal)


def local_kernel(base, head_size, decay_ref, entry_ref, readout_ref, signal_ref, gate_ref, state_in, *rest):
    inside_ref, share_ref, state_ref, in_ref, out_ref, whole_ref, step_ref = rest[-7:]
    step = pl.program_id(0)
    rows, width = signal_ref.shape
    per_tile = rows // CHUNK
    spread = spread_matrix(width, head_size)

    @pl.when(step == 0)
    def _():
        tall = stacked(decay_ref[...])
        chunks = tall.shape[0] // HEAD_ROWS
        half = CHUNK // 2
        s_from = lax.broadcasted_iota(jnp.int32, (CHUNK, CHUNK), 0)
        s_to = lax.broadcasted_iota(jnp.int32, (CHUNK, CHUNK), 1)
        first = (s_from < half).astype(F32)
        centred = ((s_from <= s_to).astype(F32) - first).astype(BF16)
        matrix = jnp.concatenate([centred, first.astype(BF16), (1.0 - first).astype(BF16)], axis=1)
        three = sums(tall, matrix)
        before = jnp.zeros((HEAD_ROWS, CHUNK), F32)
        for c in range(chunks):
            part = three[c * HEAD_ROWS : (c + 1) * HEAD_ROWS]
            from_middle = part[:, :CHUNK]
            to_middle = part[:, CHUNK : 2 * CHUNK]
            onward = part[:, 2 * CHUNK :]
            in_ref[c] = pair_rows(jnp.exp(-from_middle))
            out_ref[c] = pair_rows(jnp.exp(from_middle))
            whole_ref[c] = pair_rows(jnp.exp(before + (to_middle + from_middle)))
            if c + 1 < chunks:
                following = three[(c + 1) * HEAD_ROWS : (c + 2) * HEAD_ROWS, CHUNK : 2 * CHUNK]
                step_ref[c] = pair_rows(jnp.exp(onward + following))
            else:
                step_ref[c] = pair_rows(jnp.exp(onward))
            before = before + (to_middle + onward)
        state_ref[...] = state_in[...]

    t_row = lax.broadcasted_iota(jnp.int32, (CHUNK, CHUNK), 0)
    s_column = lax.broadcasted_iota(jnp.int32, (CHUNK, CHUNK), 1)
    causal = t_row >= s_column
    state = state_ref[...]
    for k in range(per_tile):
        c = base + step * per_tile + k
        where = pl.ds(k * CHUNK, CHUNK)
        entry = entry_ref[where, :]
        readout = readout_ref[where, :]
        scaled = (signal_ref[where, :].astype(F32) * mm(in_ref[c], spread, TN)).astype(BF16)
        scores = jnp.where(causal, mm(readout, entry, NT), 0.0).astype(BF16)
        left = jnp.concatenate([scores, readout], axis=1)
        right = jnp.concatenate([scaled, state.astype(BF16)], axis=0)
        output = mm(left, right) * mm(out_ref[c], spread, TN)
        state = state + mm(entry, scaled, TN)
        onward = mm(step_ref[c][:, :HEAD_ROWS], spread, TN)
        size = state.shape[0]
        state = (state.reshape(size // HEAD_ROWS, HEAD_ROWS, width) * onward[None]).reshape(size, width)
        gate = gate_ref[where, :].astype(F32)
        silu = gate / (1.0 + jnp.exp(-gate))
        inside_ref[where, :] = (output * silu).astype(BF16)
        share_ref[where, :] = (silu * mm(whole_ref[c], spread, TN)).astype(BF16)
    state_ref[...] = state


def local_part(index, parts, decay, entry_map, readout, signal, gate_input, state, kept, head_size, tile):
    length, width = signal.shape
    state_size = entry_map.shape[1]
    tiles = length // tile // parts
    first = index * tiles
    row_block = lambda i: (i + first, 0)
    fixed = lambda i: (0, 0)
    in_specs = [
        pl.BlockSpec((HEAD_ROWS, length), fixed),
        pl.BlockSpec((tile, state_size), row_block),
        pl.BlockSpec((tile, state_size), row_block),
        pl.BlockSpec((tile, width), row_block),
        pl.BlockSpec((tile, width), row_block),
        pl.BlockSpec((state_size, width), fixed),
    ]
    arguments = [decay, entry_map, readout, signal, gate_input, state]
    aliases = {}
    if kept is not None:
        aliases = {len(arguments): 0, len(arguments) + 1: 1}
        arguments += list(kept)
        in_specs += [pl.BlockSpec(memory_space=pl.ANY)] * 2
    chunks = length // CHUNK
    return pl.pallas_call(
        functools.partial(local_kernel, first * (tile // CHUNK), head_size),
        grid=(tiles,),
        in_specs=in_specs,
        out_specs=[
            pl.BlockSpec((tile, width), row_block),
            pl.BlockSpec((tile, width), row_block),
            pl.BlockSpec((state_size, width), fixed),
        ],
        out_shape=[
            jax.ShapeDtypeStruct((length, width), BF16),
            jax.ShapeDtypeStruct((length, width), BF16),
            jax.ShapeDtypeStruct((state_size, width), F32),
        ],
        input_output_aliases=aliases,
        scratch_shapes=[pltpu.VMEM((chunks, 2 * HEAD_ROWS, CHUNK), BF16)] * 4,
        name="local_part",
        cost_estimate=pl.CostEstimate(
            flops=8 * length * width * state_size // parts,
            bytes_accessed=2 * length * (4 * width + 2 * state_size) // parts,
            transcendentals=length * width // parts,
        ),
    )(*arguments)


def final_kernel(split, head_size, place_ref, *rest):
    count = 3 if split else 1
    incoming = rest[:count]
    readout_ref, inside_ref, share_ref, gain_ref, result_ref, terms_ref = rest[count:]
    size = readout_ref.shape[1]
    width = inside_ref.shape[1]

    def keep(value, at):
        high, low = two_terms(value)
        terms_ref[:size, at : at + value.shape[1]] = high
        terms_ref[size:, at : at + value.shape[1]] = low

    @pl.when(pl.program_id(0) == 0)
    def _():
        if split:
            one, two, kept = incoming
            place = place_ref[0]
            half = width // 2

            @pl.when(place == 1)
            def _():
                keep(kept[...], 0)
                keep(two[...], half)

            @pl.when(place == 2)
            def _():
                keep(one[...], 0)
                keep(kept[...], half)

            @pl.when((place != 1) & (place != 2))
            def _():
                keep(two[...], 0)
                keep(one[...], half)
        else:
            keep(incoming[0][...], 0)

    group = min(width, 256)
    row = lax.broadcasted_iota(jnp.int32, (group, group), 0)
    column = lax.broadcasted_iota(jnp.int32, (group, group), 1)
    same = lax.div(row, head_size) == lax.div(column, head_size)
    average = jnp.where(same, 1.0 / head_size, 0.0).astype(BF16)
    readout = readout_ref[...]
    across = mm(jnp.concatenate([readout, readout], axis=1), terms_ref[...])
    gated = inside_ref[...].astype(F32) + share_ref[...].astype(F32) * across
    squares = (gated * gated).astype(BF16)
    mean = jnp.concatenate(
        [mm(squares[:, g : g + group], average) for g in range(0, width, group)], axis=1
    )
    result_ref[...] = (gated * lax.rsqrt(mean + EPSILON) * gain_ref[...]).astype(BF16)


def final_part(place, incoming, readout, inside, share, norm_gain, head_size, split, tile):
    length, width = inside.shape
    state_size = readout.shape[1]
    row_block = lambda i: (i, 0)
    fixed = lambda i: (0, 0)
    return pl.pallas_call(
        functools.partial(final_kernel, split, head_size),
        grid=(length // tile,),
        in_specs=[pl.BlockSpec(memory_space=pltpu.SMEM)]
        + [pl.BlockSpec(v.shape, fixed) for v in incoming]
        + [
            pl.BlockSpec((tile, state_size), row_block),
            pl.BlockSpec((tile, width), row_block),
            pl.BlockSpec((tile, width), row_block),
            pl.BlockSpec((1, width), fixed),
        ],
        out_specs=pl.BlockSpec((tile, width), row_block),
        out_shape=jax.ShapeDtypeStruct((length, width), BF16),
        scratch_shapes=[pltpu.VMEM((2 * state_size, width), BF16)],
        name="final_part",
        cost_estimate=pl.CostEstimate(
            flops=4 * length * width * state_size,
            bytes_accessed=2 * length * (3 * width + state_size),
            transcendentals=length * width,
        ),
    )(place, *incoming, readout, inside, share, norm_gain)


def blend_kernel(place_ref, one_ref, two_ref, own_ref, first_ref, second_ref, kept_ref):
    size = kept_ref.shape[0]
    width = kept_ref.shape[1]

    def scaled(rows_ref, value):
        gain = rows_ref[size:, :]
        shape = (size // HEAD_ROWS, HEAD_ROWS, width)
        return (value.reshape(shape) * gain[None]).reshape(size, width)

    @pl.when(place_ref[0] == 1)
    def _():
        mine = own_ref.at[0]
        first = one_ref[:size, :]
        second = mine[:size, :] + scaled(mine, first)
        first_ref[...] = second
        second_ref[...] = two_ref[:size, :] + scaled(two_ref, second)
        kept_ref[...] = first

    @pl.when(place_ref[0] != 1)
    def _():
        mine = own_ref.at[1]
        first = two_ref[:size, :]
        second = one_ref[:size, :] + scaled(one_ref, first)
        first_ref[...] = mine[:size, :] + scaled(mine, second)
        second_ref[...] = first
        kept_ref[...] = second


def blend(place, one, two, own):
    size = one.shape[0] - HEAD_ROWS
    width = one.shape[1]
    return pl.pallas_call(
        blend_kernel,
        in_specs=[pl.BlockSpec(memory_space=pltpu.SMEM)] + [pl.BlockSpec(memory_space=pltpu.VMEM)] * 3,
        out_specs=[pl.BlockSpec(memory_space=pltpu.VMEM)] * 3,
        out_shape=[jax.ShapeDtypeStruct((size, width), F32)] * 3,
        name="blend",
    )(place, one, two, own)


def scan_devices(own, devices):
    size = own.shape[0] - HEAD_ROWS
    gain = lambda v: v[size : size + 1]
    reach, before = own, None
    shift = 1
    while shift < devices:
        came = lax.ppermute(reach, "tm", [(i, i + shift) for i in range(devices - shift)])
        join = lambda later: jnp.concatenate(
            [later[:size] + gain(later) * came[:size], later[size:] * came[size:]], axis=0
        )
        before = came if before is None else join(before)
        reach = join(reach)
        shift *= 2
    if before is None:
        return jnp.zeros_like(own[:size])
    return before[:size]


def shards(devices, signal, entry_map, readout, gate_input, log_decay, norm_gain):
    heads, length = log_decay.shape
    width = signal.shape[1]
    head_size = width // heads
    state_size = entry_map.shape[1]
    split = devices == 4 and width % 256 == 0
    tile = 512
    decay = log_decay
    if heads < HEAD_ROWS:
        decay = jnp.pad(log_decay, ((0, HEAD_ROWS - heads), (0, 0)))
    place = lax.axis_index("tm").astype(jnp.int32).reshape(1)
    made = local_states(place, decay, entry_map, signal, head_size, split, tile)
    start = jnp.zeros((state_size, width), F32)
    common = (decay, entry_map, readout, signal, gate_input)
    inside, share, state = local_part(0, 2, *common, start, None, head_size, tile)
    if split:
        own, first, second = made
        one = lax.ppermute(first, "tm", [(0, 1), (1, 2)])
        two = lax.ppermute(second, "tm", [(2, 1), (0, 2)])
        first, second, kept = blend(place, one, two, own)
        one = lax.ppermute(first, "tm", [(1, 2), (2, 3)])
        two = lax.ppermute(second, "tm", [(1, 3), (2, 1)])
        incoming = (one, two, kept)
    else:
        incoming = (scan_devices(made[0], devices),)
    inside, share, state = local_part(1, 2, *common, state, (inside, share), head_size, tile)
    return final_part(
        place, incoming, readout, inside, share, norm_gain.reshape(1, width), head_size, split, tile
    )


def solution(mesh):
    in_specs = (
        P(("parts", "tm"), ("head", "sub")),
        P(("parts", "tm"), None),
        P(("parts", "tm"), None),
        P(("parts", "tm"), ("head", "sub")),
        P(("head", "sub"), ("parts", "tm")),
        P(("head", "sub")),
    )
    out_specs = P(("parts", "tm"), ("head", "sub"))
    body = functools.partial(shards, mesh.shape["tm"])
    return jax.shard_map(body, mesh=mesh, in_specs=in_specs, out_specs=out_specs, check_vma=False)
```

time: 319 us -> 57.6 us (0.18)
  the two profiles are of different devices: /device:TPU:0 before, /device:TPU:16 now
where the time goes in v1:
time: 57.6 us; the launch traced here: 56.9 us
  Pallas kernels  38.4 us (67%)
  starting transfers between devices  11.7 us (20%)
  waiting for transfers between devices  4.65 us (8%)
  local copies, waits for them, and re-layouts  2.12 us (4%)
    pallas_call x2, Pallas kernels, local_part(): pl.pallas_call(functools.partial(local_kernel, first * (tile // CHUNK), h...  18.3 us
    pallas_call x1, Pallas kernels, final_part(): pl.pallas_call(functools.partial(final_kernel, split, head_size), grid=(l...  9.59 us
    pallas_call x1, Pallas kernels, local_states(): pl.pallas_call(functools.partial(state_kernel, split, head_size), grid=(l...  8.56 us
    ppermute x1, waiting for transfers between devices, shards(): one = lax.ppermute(first, 'tm', [(0, 1), (1, 2)])  4.64 us
    ppermute x1, starting transfers between devices, shards(): two = lax.ppermute(second, 'tm', [(2, 1), (0, 2)])  4.55 us
    ppermute x1, starting transfers between devices, shards(): two = lax.ppermute(second, 'tm', [(1, 3), (2, 1)])  3.93 us
    pallas_call x1, Pallas kernels, blend(): pl.pallas_call(blend_kernel, in_specs=[pl.BlockSpec(memory_space=pltpu.SM...  1.92 us
    ppermute x1, starting transfers between devices, shards(): one = lax.ppermute(first, 'tm', [(1, 2), (2, 3)])  1.91 us
  transfers between devices with their start and end apart: 4, of which 1 were waited for; matrix products, arithmetic and copies ran while one was open for 1% of the time, Pallas kernels for 32%

profile of v1, /device:TPU:16, one launch (start us, length us, event | category | flops | bytes accessed | tf_op | source)
XLA Modules:
  0.0 56.9 jit_solution(242088858779260264)
XLA Ops:
  0.0 8.6 %device_states.1 = (f32[2,136,256]{2,1,0:T(8,128)}, f32[136,256]{1,0:T(8,128)}, f32[136,256]{1,0:T(8,128)}) custom-call(s32[1]{0:T(128)} %bitcast.place_ref, f32[8,4096]{1,0:T(8,128)} %decay_ref.5, bf16[4096,128]{1,0:T(8,128)(2,1)} %entry_ref.5, bf16[4096,512]{1,0:T(8,128)(2,1)} %signal_ref.5), custom_call_target="tpu_custom_call" | custom-call | flops 536870912 | bytes 5242880 | tf_op jit(solution)/shard_map/device_states/pallas_call | solution.py:128
  8.6 1.3 %collective-permute-start = (f32[136,256]{1,0:T(8,128)}, f32[136,256]{1,0:T(8,128)S(1)}, u32[]{:S(2)}, u32[]{:S(2)}) collective-permute-start(f32[136,256]{1,0:T(8,128)} %get-tuple-element.16), channel_id=1, source_target_pairs={{0,4},{4,8},{1,5},{5,9},{2,6},{6,10},{3,7},{7,11},{16,20},{20,24},... | collective-permute-start | bytes 417800 | tf_op jit(solution)/shard_map/ppermute | solution.py:414
  9.9 4.5 %collective-permute-start.1 = (f32[136,256]{1,0:T(8,128)}, f32[136,256]{1,0:T(8,128)S(1)}, u32[]{:S(2)}, u32[]{:S(2)}) collective-permute-start(f32[136,256]{1,0:T(8,128)} %get-tuple-element.17), channel_id=1, source_target_pairs={{8,4},{0,8},{9,5},{1,9},{10,6},{2,10},{11,7},{3,11},{24,20},{16,24... | collective-permute-start | bytes 417800 | tf_op jit(solution)/shard_map/ppermute | solution.py:415
  14.4 4.6 %collective-permute-done.one_ref = f32[136,256]{1,0:T(8,128)S(1)} collective-permute-done((f32[136,256]{1,0:T(8,128)}, f32[136,256]{1,0:T(8,128)S(1)}, u32[]{:S(2)}, u32[]{:S(2)}) %collective-permute-start) | collective-permute-done | bytes 139296 | tf_op jit(solution)/shard_map/ppermute | solution.py:414
  19.1 0.0 copy-start
  19.1 0.0 collective-permute-done.1.two_ref
  19.1 0.0 copy-start.1
  19.1 0.6 %copy-done = f32[136,256]{1,0:T(8,128)} copy-done((f32[136,256]{1,0:T(8,128)}, f32[136,256]{1,0:T(8,128)S(1)}, u32[]{:S(2)}) %copy-start) | copy-done | bytes 139288
  19.7 0.1 copy-done.1
  19.8 1.9 %blend.1 = (f32[128,256]{1,0:T(8,128)}, f32[128,256]{1,0:T(8,128)}, f32[128,256]{1,0:T(8,128)}) custom-call(s32[1]{0:T(128)} %bitcast.place_ref, f32[136,256]{1,0:T(8,128)} %copy-done, f32[136,256]{1,0:T(8,128)} %copy-done.1, f32[2,136,256]{2,1,0:T(8,128)} %get-tuple-element.18.own_ref), custom_call_target="tpu_custom_call" | custom-call | tf_op jit(solution)/shard_map/blend/pallas_call | solution.py:370
  21.7 1.9 %collective-permute-start.2 = (f32[128,256]{1,0:T(8,128)}, f32[128,256]{1,0:T(8,128)S(1)}, u32[]{:S(2)}, u32[]{:S(2)}) collective-permute-start(f32[128,256]{1,0:T(8,128)} %get-tuple-element.19), channel_id=1, source_target_pairs={{4,8},{8,12},{5,9},{9,13},{6,10},{10,14},{7,11},{11,15},{20,24},{2... | collective-permute-start | bytes 393224 | tf_op jit(solution)/shard_map/ppermute | solution.py:417
  23.6 3.9 %collective-permute-start.3 = (f32[128,256]{1,0:T(8,128)}, f32[128,256]{1,0:T(8,128)S(1)}, u32[]{:S(2)}, u32[]{:S(2)}) collective-permute-start(f32[128,256]{1,0:T(8,128)} %get-tuple-element.20), channel_id=1, source_target_pairs={{4,12},{8,4},{5,13},{9,5},{6,14},{10,6},{7,15},{11,7},{20,28},{24,... | collective-permute-start | bytes 393224 | tf_op jit(solution)/shard_map/ppermute | solution.py:418
  27.5 0.7 %broadcast_in_dim.3.state_in = f32[128,512]{1,0:T(8,128)} broadcast(f32[]{:T(128)} %constant.6.clone.1), dimensions={} | broadcast | bytes 262148 | tf_op jit(solution)/shard_map/broadcast_in_dim | solution.py:409
  28.3 9.1 %local_part.2 = (bf16[4096,512]{1,0:T(8,128)(2,1)}, bf16[4096,512]{1,0:T(8,128)(2,1)}, f32[128,512]{1,0:T(8,128)}) custom-call(f32[8,4096]{1,0:T(8,128)} %decay_ref.5, bf16[4096,128]{1,0:T(8,128)(2,1)} %entry_ref.5, bf16[4096,128]{1,0:T(8,128)(2,1)} %rest_3_.1, bf16[4096,512]{1,0:T(8,128)(2,1)} %signal_ref.5, bf16[4096,512]{1,0:T(8,128)(2,1)} %gate_ref.3, ...), custom_call_target="tpu_custom_call" | custom-call | flops 1073741824 | bytes 9437184 | tf_op jit(solution)/shard_map/local_part/pallas_call | solution.py:235
  37.4 9.2 %local_part.3 = (bf16[4096,512]{1,0:T(8,128)(2,1)}, bf16[4096,512]{1,0:T(8,128)(2,1)}, f32[128,512]{1,0:T(8,128)}) custom-call(f32[8,4096]{1,0:T(8,128)} %decay_ref.5, bf16[4096,128]{1,0:T(8,128)(2,1)} %entry_ref.5, bf16[4096,128]{1,0:T(8,128)(2,1)} %rest_3_.1, bf16[4096,512]{1,0:T(8,128)(2,1)} %signal_ref.5, ...), custom_call_target="tpu_custom_call", output_to_operand_aliasing={{0}: (6, {}), {1}: (7, {})} | custom-call | flops 1073741824 | bytes 9437184 | tf_op jit(solution)/shard_map/local_part/pallas_call | solution.py:235
  46.6 0.0 collective-permute-done.2.rest_0_
  46.6 0.0 copy-start.2
  46.6 0.0 collective-permute-done.3.rest_1_
  46.6 0.0 copy-start.3
  46.6 0.6 %copy-done.2 = f32[128,256]{1,0:T(8,128)} copy-done((f32[128,256]{1,0:T(8,128)}, f32[128,256]{1,0:T(8,128)S(1)}, u32[]{:S(2)}) %copy-start.2) | copy-done | bytes 131096
  47.2 0.1 copy-done.3
  47.3 9.6 %final_part.1 = bf16[4096,512]{1,0:T(8,128)(2,1)} custom-call(s32[1]{0:T(128)} %bitcast.place_ref, f32[128,256]{1,0:T(8,128)} %copy-done.2, f32[128,256]{1,0:T(8,128)} %copy-done.3, f32[128,256]{1,0:T(8,128)} %get-tuple-element.21.rest_2_, bf16[4096,128]{1,0:T(8,128)(2,1)} %rest_3_.1, bf16[4096,512]{1,0:T(8,128)(2,1)} %get-tuple-element.25.rest_4_, ...), custom_call_target="tpu_custom_call" | custom-call | flops 1073741824 | bytes 13631488 | tf_op jit(solution)/shard_map/final_part/pallas_call | solution.py:316
Async XLA Ops:
  8.6 10.5 %collective-permute-start = (f32[136,256]{1,0:T(8,128)}, f32[136,256]{1,0:T(8,128)S(1)}, u32[]{:S(2)}, u32[]{:S(2)}) collective-permute-start(f32[136,256]{1,0:T(8,128)} %get-tuple-element.16), channel_id=1, source_target_pairs={{0,4},{4,8},{1,5},{5,9},{2,6},{6,10},{3,7},{7,11},{16,20},{20,24},... | collective-permute-start | bytes 417800 | tf_op jit(solution)/shard_map/ppermute | solution.py:414
  9.9 9.2 %collective-permute-start.1 = (f32[136,256]{1,0:T(8,128)}, f32[136,256]{1,0:T(8,128)S(1)}, u32[]{:S(2)}, u32[]{:S(2)}) collective-permute-start(f32[136,256]{1,0:T(8,128)} %get-tuple-element.17), channel_id=1, source_target_pairs={{8,4},{0,8},{9,5},{1,9},{10,6},{2,10},{11,7},{3,11},{24,20},{16,24... | collective-permute-start | bytes 417800 | tf_op jit(solution)/shard_map/ppermute | solution.py:415
  19.1 0.6 %copy-start = (f32[136,256]{1,0:T(8,128)}, f32[136,256]{1,0:T(8,128)S(1)}, u32[]{:S(2)}) copy-start(f32[136,256]{1,0:T(8,128)S(1)} %collective-permute-done.one_ref) | copy-start | bytes 417796
  19.1 0.7 %copy-start.1 = (f32[136,256]{1,0:T(8,128)}, f32[136,256]{1,0:T(8,128)S(1)}, u32[]{:S(2)}) copy-start(f32[136,256]{1,0:T(8,128)S(1)} %collective-permute-done.1.two_ref) | copy-start | bytes 417796
  21.7 24.9 %collective-permute-start.2 = (f32[128,256]{1,0:T(8,128)}, f32[128,256]{1,0:T(8,128)S(1)}, u32[]{:S(2)}, u32[]{:S(2)}) collective-permute-start(f32[128,256]{1,0:T(8,128)} %get-tuple-element.19), channel_id=1, source_target_pairs={{4,8},{8,12},{5,9},{9,13},{6,10},{10,14},{7,11},{11,15},{20,24},{2... | collective-permute-start | bytes 393224 | tf_op jit(solution)/shard_map/ppermute | solution.py:417
  23.6 23.0 %collective-permute-start.3 = (f32[128,256]{1,0:T(8,128)}, f32[128,256]{1,0:T(8,128)S(1)}, u32[]{:S(2)}, u32[]{:S(2)}) collective-permute-start(f32[128,256]{1,0:T(8,128)} %get-tuple-element.20), channel_id=1, source_target_pairs={{4,12},{8,4},{5,13},{9,5},{6,14},{10,6},{7,15},{11,7},{20,28},{24,... | collective-permute-start | bytes 393224 | tf_op jit(solution)/shard_map/ppermute | solution.py:418
  46.6 0.7 %copy-start.2 = (f32[128,256]{1,0:T(8,128)}, f32[128,256]{1,0:T(8,128)S(1)}, u32[]{:S(2)}) copy-start(f32[128,256]{1,0:T(8,128)S(1)} %collective-permute-done.2.rest_0_) | copy-start | bytes 393220
  46.6 0.7 %copy-start.3 = (f32[128,256]{1,0:T(8,128)}, f32[128,256]{1,0:T(8,128)S(1)}, u32[]{:S(2)}) copy-start(f32[128,256]{1,0:T(8,128)S(1)} %collective-permute-done.3.rest_1_) | copy-start | bytes 393220

commit v2 on v1

v2 whole, which is shorter than its diff:
```python
import functools

import jax
import jax.numpy as jnp
from jax import lax
from jax.experimental import pallas as pl
from jax.experimental.pallas import tpu as pltpu
from jax.sharding import PartitionSpec as P

CHUNK = 128
HEAD_ROWS = 8
EPSILON = 1e-05
F32 = jnp.float32
BF16 = jnp.bfloat16
TN = (((0,), (0,)), ((), ()))
NT = (((1,), (1,)), ((), ()))
IN_HBM = pl.BlockSpec(memory_space=pltpu.HBM)
IN_VMEM = pl.BlockSpec(memory_space=pltpu.VMEM)


def mm(left, right, dims=(((1,), (0,)), ((), ()))):
    return lax.dot_general(left, right, dims, preferred_element_type=F32)


def two_terms(value):
    high = value.astype(BF16)
    return high, (value - high.astype(F32)).astype(BF16)


def spread_matrix(width, head_size):
    row = lax.broadcasted_iota(jnp.int32, (2 * HEAD_ROWS, width), 0)
    column = lax.broadcasted_iota(jnp.int32, (2 * HEAD_ROWS, width), 1)
    own = lax.rem(row, HEAD_ROWS) == lax.div(column, head_size)
    return own.astype(F32).astype(BF16)


def stacked(decay):
    chunks = decay.shape[1] // CHUNK
    return jnp.concatenate([decay[:, c * CHUNK : (c + 1) * CHUNK] for c in range(chunks)], axis=0)


def sums(decay_rows, matrix):
    high = decay_rows.astype(BF16)
    rest = decay_rows - high.astype(F32)
    middle = rest.astype(BF16)
    low = (rest - middle.astype(F32)).astype(BF16)
    return mm(high, matrix) + (mm(middle, matrix) + mm(low, matrix))


def pair_rows(value):
    high, low = two_terms(value)
    return jnp.concatenate([high, low], axis=0)


def indicator(test):
    return test.astype(F32).astype(BF16)


def copy_rows(source, target, semaphore, start, rows):
    where = pl.ds(start, rows)
    return pltpu.make_async_copy(source.at[where], target.at[where], semaphore)


def state_kernel(split, head_size, pieces, place_ref, decay_hbm, entry_hbm, signal_hbm, *rest):
    outs, (entry_ref, signal_ref, decay_ref, factor_ref, semaphores) = rest[:-5], rest[-5:]
    length, width = signal_ref.shape
    rows = length // pieces
    chunks = length // CHUNK
    decay_copy = pltpu.make_async_copy(decay_hbm, decay_ref, semaphores.at[2 * pieces])
    decay_copy.start()
    copies = []
    for k in range(pieces):
        copies.append(copy_rows(entry_hbm, entry_ref, semaphores.at[k], k * rows, rows))
        copies.append(copy_rows(signal_hbm, signal_ref, semaphores.at[pieces + k], k * rows, rows))
    for copy in copies:
        copy.start()
    spread = spread_matrix(width, head_size)
    decay_copy.wait()
    tall = stacked(decay_ref[...])
    s_from = lax.broadcasted_iota(jnp.int32, (CHUNK, 2 * CHUNK), 0)
    s_to = lax.broadcasted_iota(jnp.int32, (CHUNK, 2 * CHUNK), 1)
    both = sums(tall, indicator((s_from > s_to) | (s_to >= CHUNK)))
    later = jnp.zeros((HEAD_ROWS, CHUNK), F32)
    for c in reversed(range(chunks)):
        part = both[c * HEAD_ROWS : (c + 1) * HEAD_ROWS]
        factor_ref[c] = pair_rows(jnp.exp(part[:, :CHUNK] + later))
        later = later + part[:, CHUNK:]
    gain = mm(pair_rows(jnp.exp(later[:, :HEAD_ROWS])), spread, TN)
    states = None
    for k in range(pieces):
        copies[2 * k].wait()
        copies[2 * k + 1].wait()
        for start in range(k * rows, (k + 1) * rows, 2 * CHUNK):
            where = pl.ds(start, 2 * CHUNK)
            c = start // CHUNK
            factor = jnp.concatenate([mm(factor_ref[c + j], spread, TN) for j in range(2)], axis=0)
            scaled = (signal_ref[where, :].astype(F32) * factor).astype(BF16)
            term = mm(entry_ref[where, :], scaled, TN)
            states = term if states is None else states + term
    size = states.shape[0]
    if split:
        own_ref, first_ref, second_ref = outs
        half = width // 2
        for k in range(2):
            own_ref[k, :size, :] = states[:, k * half : (k + 1) * half]
            own_ref[k, size:, :] = gain[:, k * half : (k + 1) * half]

        @pl.when(place_ref[0] == 0)
        def _():
            first_ref[...] = own_ref[0]
            second_ref[...] = own_ref[1]

        @pl.when(place_ref[0] != 0)
        def _():
            first_ref[...] = own_ref[1]
            second_ref[...] = own_ref[0]
    else:
        (own_ref,) = outs
        own_ref[:size, :] = states
        own_ref[size:, :] = gain


def local_states(place, decay, entry_map, signal, head_size, split, pieces):
    length, width = signal.shape
    state_size = entry_map.shape[1]
    tall = state_size + HEAD_ROWS
    if split:
        shapes = [(2, tall, width // 2), (tall, width // 2), (tall, width // 2)]
    else:
        shapes = [(tall, width)]
    return pl.pallas_call(
        functools.partial(state_kernel, split, head_size, pieces),
        in_specs=[pl.BlockSpec(memory_space=pltpu.SMEM)] + [IN_HBM] * 3,
        out_specs=[IN_VMEM] * (len(shapes) + 2),
        out_shape=[pltpu.VMEM(s, F32) for s in shapes]
        + [pltpu.VMEM((length, state_size), BF16), pltpu.VMEM((length, width), BF16)],
        scratch_shapes=[
            pltpu.VMEM((HEAD_ROWS, length), F32),
            pltpu.VMEM((length // CHUNK, 2 * HEAD_ROWS, CHUNK), BF16),
            pltpu.SemaphoreType.DMA((2 * pieces + 1,)),
        ],
        name="device_states",
        compiler_params=pltpu.CompilerParams(vmem_limit_bytes=16 << 20),
        cost_estimate=pl.CostEstimate(
            flops=2 * length * width * state_size,
            bytes_accessed=2 * length * (width + state_size),
            transcendentals=0,
        ),
    )(place, decay, entry_map, signal)


def local_kernel(base, head_size, pieces, decay_hbm, readout_hbm, gate_hbm, gain_hbm, entry_ref, signal_ref, state_in, *rest):
    inside_ref, share_ref, readout_ref, gain_ref, state_ref = rest[:5]
    decay_ref, gate_ref, in_ref, out_ref, whole_ref, step_ref, semaphores = rest[5:]
    length, width = signal_ref.shape
    part_rows = inside_ref.shape[0]
    rows = part_rows // pieces
    chunks = length // CHUNK
    decay_copy = pltpu.make_async_copy(decay_hbm, decay_ref, semaphores.at[0])
    readout_copy = pltpu.make_async_copy(readout_hbm.at[pl.ds(base, part_rows)], readout_ref, semaphores.at[1])
    gain_copy = pltpu.make_async_copy(gain_hbm, gain_ref, semaphores.at[2])
    gate_copies = [
        pltpu.make_async_copy(
            gate_hbm.at[pl.ds(base + k * rows, rows)], gate_ref.at[pl.ds(k * rows, rows)], semaphores.at[3 + k]
        )
        for k in range(pieces)
    ]
    decay_copy.start()
    readout_copy.start()
    for copy in gate_copies:
        copy.start()
    gain_copy.start()
    spread = spread_matrix(width, head_size)
    decay_copy.wait()
    tall = stacked(decay_ref[...])
    half = CHUNK // 2
    s_from = lax.broadcasted_iota(jnp.int32, (CHUNK, CHUNK), 0)
    s_to = lax.broadcasted_iota(jnp.int32, (CHUNK, CHUNK), 1)
    early = (s_from < half).astype(F32)
    centred = ((s_from <= s_to).astype(F32) - early).astype(BF16)
    matrix = jnp.concatenate([centred, early.astype(BF16), (1.0 - early).astype(BF16)], axis=1)
    three = sums(tall, matrix)
    before = jnp.zeros((HEAD_ROWS, CHUNK), F32)
    for c in range(chunks):
        part = three[c * HEAD_ROWS : (c + 1) * HEAD_ROWS]
        from_middle = part[:, :CHUNK]
        to_middle = part[:, CHUNK : 2 * CHUNK]
        onward = part[:, 2 * CHUNK :]
        if base <= c * CHUNK < base + part_rows:
            in_ref[c] = pair_rows(jnp.exp(-from_middle))
            out_ref[c] = pair_rows(jnp.exp(from_middle))
            whole_ref[c] = pair_rows(jnp.exp(before + (to_middle + from_middle)))
            if c + 1 < chunks:
                following = three[(c + 1) * HEAD_ROWS : (c + 2) * HEAD_ROWS, CHUNK : 2 * CHUNK]
                step_ref[c] = pair_rows(jnp.exp(onward + following))
            else:
                step_ref[c] = pair_rows(jnp.exp(onward))
        before = before + (to_middle + onward)
    t_row = lax.broadcasted_iota(jnp.int32, (CHUNK, CHUNK), 0)
    s_column = lax.broadcasted_iota(jnp.int32, (CHUNK, CHUNK), 1)
    causal = t_row >= s_column
    state = state_in[...] if base else jnp.zeros(state_ref.shape, F32)
    readout_copy.wait()
    for k in range(part_rows // CHUNK):
        if k % (rows // CHUNK) == 0:
            gate_copies[k // (rows // CHUNK)].wait()
        c = base // CHUNK + k
        here = pl.ds(k * CHUNK, CHUNK)
        where = pl.ds(c * CHUNK, CHUNK)
        entry = entry_ref[where, :]
        readout = readout_ref[here, :]
        scaled = (signal_ref[where, :].astype(F32) * mm(in_ref[c], spread, TN)).astype(BF16)
        scores = jnp.where(causal, mm(readout, entry, NT), 0.0).astype(BF16)
        left = jnp.concatenate([scores, readout], axis=1)
        right = jnp.concatenate([scaled, state.astype(BF16)], axis=0)
        output = mm(left, right) * mm(out_ref[c], spread, TN)
        state = state + mm(entry, scaled, TN)
        onward = mm(step_ref[c][:, :HEAD_ROWS], spread, TN)
        size = state.shape[0]
        state = (state.reshape(size // HEAD_ROWS, HEAD_ROWS, width) * onward[None]).reshape(size, width)
        gate = gate_ref[here, :].astype(F32)
        silu = gate / (1.0 + jnp.exp(-gate))
        inside_ref[here, :] = (output * silu).astype(BF16)
        share_ref[here, :] = (silu * mm(whole_ref[c], spread, TN)).astype(BF16)
    state_ref[...] = state
    gain_copy.wait()


def local_part(index, parts, decay, readout, gate_input, norm_gain, entry_map, signal, state, head_size, pieces):
    length, width = signal.shape
    state_size = entry_map.shape[1]
    rows = length // parts
    chunks = length // CHUNK
    return pl.pallas_call(
        functools.partial(local_kernel, index * rows, head_size, pieces),
        in_specs=[IN_HBM] * 4 + [IN_VMEM] * 3,
        out_specs=[IN_VMEM] * 5,
        out_shape=[
            pltpu.VMEM((rows, width), BF16),
            pltpu.VMEM((rows, width), BF16),
            pltpu.VMEM((rows, state_size), BF16),
            pltpu.VMEM((1, width), F32),
            pltpu.VMEM((state_size, width), F32),
        ],
        scratch_shapes=[pltpu.VMEM((HEAD_ROWS, length), F32), pltpu.VMEM((rows, width), BF16)]
        + [pltpu.VMEM((chunks, 2 * HEAD_ROWS, CHUNK), BF16)] * 4
        + [pltpu.SemaphoreType.DMA((3 + pieces,))],
        name="local_part",
        compiler_params=pltpu.CompilerParams(vmem_limit_bytes=16 << 20),
        cost_estimate=pl.CostEstimate(
            flops=8 * length * width * state_size // parts,
            bytes_accessed=2 * length * (4 * width + 2 * state_size) // parts,
            transcendentals=length * width // parts,
        ),
    )(decay, readout, gate_input, norm_gain, entry_map, signal, state)


def final_kernel(split, head_size, parts, rows, place_ref, *rest):
    count = 3 if split else 1
    incoming, rest = rest[:count], rest[count:]
    groups = [rest[3 * p : 3 * p + 3] for p in range(parts)]
    gain_ref, result_hbm, result_ref, terms_ref, semaphores = rest[3 * parts :]
    size = groups[0][0].shape[1]
    part_rows, width = groups[0][1].shape

    def keep(value, at):
        high, low = two_terms(value)
        terms_ref[:size, at : at + value.shape[1]] = high
        terms_ref[size:, at : at + value.shape[1]] = low

    if split:
        one, two, kept = incoming
        place = place_ref[0]
        half = width // 2

        @pl.when(place == 1)
        def _():
            keep(kept[...], 0)
            keep(two[...], half)

        @pl.when(place == 2)
        def _():
            keep(one[...], 0)
            keep(kept[...], half)

        @pl.when((place != 1) & (place != 2))
        def _():
            keep(two[...], 0)
            keep(one[...], half)
    else:
        keep(incoming[0][...], 0)

    group = min(width, 256)
    row = lax.broadcasted_iota(jnp.int32, (group, group), 0)
    column = lax.broadcasted_iota(jnp.int32, (group, group), 1)
    same = lax.div(row, head_size) == lax.div(column, head_size)
    average = jnp.where(same, 1.0 / head_size, 0.0).astype(BF16)
    gain = gain_ref[...]
    copies = []
    for p, (readout_ref, inside_ref, share_ref) in enumerate(groups):
        for start in range(0, part_rows, rows):
            where = pl.ds(start, rows)
            there = pl.ds(p * part_rows + start, rows)
            readout = readout_ref[where, :]
            across = mm(jnp.concatenate([readout, readout], axis=1), terms_ref[...])
            gated = inside_ref[where, :].astype(F32) + share_ref[where, :].astype(F32) * across
            squares = (gated * gated).astype(BF16)
            mean = jnp.concatenate(
                [mm(squares[:, g : g + group], average) for g in range(0, width, group)], axis=1
            )
            result_ref[there, :] = (gated * lax.rsqrt(mean + EPSILON) * gain).astype(BF16)
            copy = pltpu.make_async_copy(result_ref.at[there], result_hbm.at[there], semaphores.at[len(copies)])
            copy.start()
            copies.append(copy)
    for copy in copies:
        copy.wait()


def final_part(place, incoming, groups, norm_gain, head_size, split, rows):
    part_rows, width = groups[0][1].shape
    length = part_rows * len(groups)
    state_size = groups[0][0].shape[1]
    return pl.pallas_call(
        functools.partial(final_kernel, split, head_size, len(groups), rows),
        in_specs=[pl.BlockSpec(memory_space=pltpu.SMEM)]
        + [IN_VMEM] * (len(incoming) + 3 * len(groups) + 1),
        out_specs=IN_HBM,
        out_shape=jax.ShapeDtypeStruct((length, width), BF16),
        scratch_shapes=[
            pltpu.VMEM((length, width), BF16),
            pltpu.VMEM((2 * state_size, width), BF16),
            pltpu.SemaphoreType.DMA((length // rows,)),
        ],
        name="final_part",
        compiler_params=pltpu.CompilerParams(vmem_limit_bytes=16 << 20),
        cost_estimate=pl.CostEstimate(
            flops=4 * length * width * state_size,
            bytes_accessed=2 * length * (3 * width + state_size),
            transcendentals=length * width,
        ),
    )(place, *incoming, *[v for g in groups for v in g], norm_gain)


def blend_kernel(place_ref, one_ref, two_ref, own_ref, first_ref, second_ref, kept_ref):
    size = kept_ref.shape[0]
    width = kept_ref.shape[1]

    def scaled(rows_ref, value):
        gain = rows_ref[size:, :]
        shape = (size // HEAD_ROWS, HEAD_ROWS, width)
        return (value.reshape(shape) * gain[None]).reshape(size, width)

    @pl.when(place_ref[0] == 1)
    def _():
        mine = own_ref.at[0]
        first = one_ref[:size, :]
        second = mine[:size, :] + scaled(mine, first)
        first_ref[...] = second
        second_ref[...] = two_ref[:size, :] + scaled(two_ref, second)
        kept_ref[...] = first

    @pl.when(place_ref[0] != 1)
    def _():
        mine = own_ref.at[1]
        first = two_ref[:size, :]
        second = one_ref[:size, :] + scaled(one_ref, first)
        first_ref[...] = mine[:size, :] + scaled(mine, second)
        second_ref[...] = first
        kept_ref[...] = second


def blend(place, one, two, own):
    size = one.shape[0] - HEAD_ROWS
    width = one.shape[1]
    return pl.pallas_call(
        blend_kernel,
        in_specs=[pl.BlockSpec(memory_space=pltpu.SMEM)] + [IN_VMEM] * 3,
        out_specs=[IN_VMEM] * 3,
        out_shape=[pltpu.VMEM((size, width), F32)] * 3,
        name="blend",
        compiler_params=pltpu.CompilerParams(vmem_limit_bytes=4 << 20),
    )(place, one, two, own)


def scan_devices(own, devices):
    size = own.shape[0] - HEAD_ROWS
    gain = lambda v: v[size : size + 1]
    reach, before = own, None
    shift = 1
    while shift < devices:
        came = lax.ppermute(reach, "tm", [(i, i + shift) for i in range(devices - shift)])
        join = lambda later: jnp.concatenate(
            [later[:size] + gain(later) * came[:size], later[size:] * came[size:]], axis=0
        )
        before = came if before is None else join(before)
        reach = join(reach)
        shift *= 2
    if before is None:
        return jnp.zeros_like(own[:size])
    return before[:size]


def shards(devices, signal, entry_map, readout, gate_input, log_decay, norm_gain):
    heads, length = log_decay.shape
    width = signal.shape[1]
    head_size = width // heads
    split = devices == 4 and width % 256 == 0
    decay = log_decay
    if heads < HEAD_ROWS:
        decay = jnp.pad(log_decay, ((0, HEAD_ROWS - heads), (0, 0)))
    place = lax.axis_index("tm").astype(jnp.int32).reshape(1)
    *made, entry_map, signal = local_states(place, decay, entry_map, signal, head_size, split, 4)
    common = (decay, readout, gate_input, norm_gain.reshape(1, width), entry_map, signal)
    nothing = jnp.zeros((8, 128), F32)
    if split:
        own, first, second = made
        one = lax.ppermute(first, "tm", [(0, 1), (1, 2)])
        two = lax.ppermute(second, "tm", [(2, 1), (0, 2)])
    inside_a, share_a, readout_a, _, state = local_part(0, 2, *common, nothing, head_size, 2)
    if split:
        one, two, state = lax.optimization_barrier((one, two, state))
        first, second, kept = blend(place, one, two, own)
        one = lax.ppermute(first, "tm", [(1, 2), (2, 3)])
        two = lax.ppermute(second, "tm", [(1, 3), (2, 1)])
        incoming = (one, two, kept)
    else:
        incoming = (scan_devices(made[0], devices),)
    inside_b, share_b, readout_b, gain, _ = local_part(1, 2, *common, state, head_size, 2)
    groups = ((readout_a, inside_a, share_a), (readout_b, inside_b, share_b))
    return final_part(place, incoming, groups, gain, head_size, split, 512)


def solution(mesh):
    in_specs = (
        P(("parts", "tm"), ("head", "sub")),
        P(("parts", "tm"), None),
        P(("parts", "tm"), None),
        P(("parts", "tm"), ("head", "sub")),
        P(("head", "sub"), ("parts", "tm")),
        P(("head", "sub")),
    )
    out_specs = P(("parts", "tm"), ("head", "sub"))
    body = functools.partial(shards, mesh.shape["tm"])
    return jax.shard_map(body, mesh=mesh, in_specs=in_specs, out_specs=out_specs, check_vma=False)
```

time: 57.6 us -> 40.7 us (0.71)
  the two profiles are of different devices: /device:TPU:16 before, /device:TPU:18 now
where the time goes in v2:
time: 40.7 us; the launch traced here: 40.5 us
  Pallas kernels  23.6 us (58%)
  starting transfers between devices  11.9 us (29%)
  local copies, waits for them, and re-layouts  4.67 us (11%)
    pallas_call x2, Pallas kernels, local_part(): pl.pallas_call(functools.partial(local_kernel, index * rows, head_size, p...  14.1 us
    pallas_call x1, Pallas kernels, local_states(): pl.pallas_call(functools.partial(state_kernel, split, head_size, pieces),...  5.25 us
    unnamed x12, local copies, waits for them, and re-layouts  4.67 us
    ppermute x1, starting transfers between devices, shards(): two = lax.ppermute(second, 'tm', [(2, 1), (0, 2)])  4.55 us
    pallas_call x1, Pallas kernels, final_part(): pl.pallas_call(functools.partial(final_kernel, split, head_size, len(grou...  4.22 us
    ppermute x1, starting transfers between devices, shards(): two = lax.ppermute(second, 'tm', [(1, 3), (2, 1)])  4.11 us
    ppermute x1, starting transfers between devices, shards(): one = lax.ppermute(first, 'tm', [(1, 2), (2, 3)])  1.92 us
    ppermute x1, starting transfers between devices, shards(): one = lax.ppermute(first, 'tm', [(0, 1), (1, 2)])  1.29 us
  transfers between devices with their start and end apart: 4, of which 0 were waited for; matrix products, arithmetic and copies ran while one was open for 0% of the time, Pallas kernels for 35%

profile of v2, /device:TPU:18, one launch (start us, length us, event | category | flops | bytes accessed | tf_op | source)
XLA Modules:
  0.0 40.5 jit_solution(12643167652188822433)
XLA Ops:
  0.0 0.0 copy-start.5
  0.0 0.0 copy-start
  0.0 0.0 copy-start.1
  0.0 2.3 %copy-done.1 = bf16[4096,512]{1,0:T(8,128)(2,1)S(1)} copy-done((bf16[4096,512]{1,0:T(8,128)(2,1)S(1)}, bf16[4096,512]{1,0:T(8,128)(2,1)}, u32[]{:S(2)}) %copy-start.1) | copy-done | bytes 4194328
  2.3 0.0 copy-start.3
  2.3 1.1 %copy-done.3 = f32[8,4096]{1,0:T(8,128)S(1)} copy-done((f32[8,4096]{1,0:T(8,128)S(1)}, f32[8,4096]{1,0:T(8,128)}, u32[]{:S(2)}) %copy-start.3) | copy-done | bytes 131096
  3.4 0.0 copy-start.4
  3.4 1.2 %copy-done.4 = bf16[4096,128]{1,0:T(8,128)(2,1)S(1)} copy-done((bf16[4096,128]{1,0:T(8,128)(2,1)S(1)}, bf16[4096,128]{1,0:T(8,128)(2,1)}, u32[]{:S(2)}) %copy-start.4) | copy-done | bytes 1048600
  4.7 0.0 copy-start.2
  4.7 5.2 %device_states.1 = (f32[2,136,256]{2,1,0:T(8,128)S(1)}, f32[136,256]{1,0:T(8,128)S(1)}, f32[136,256]{1,0:T(8,128)S(1)}, bf16[4096,128]{1,0:T(8,128)(2,1)S(1)}, bf16[4096,512]{1,0:T(8,128)(2,1)S(1)}) custom-call(s32[1]{0:T(128)} %bitcast.place_ref, f32[8,4096]{1,0:T(8,128)S(1)} %copy-done.3, bf16[4096,128]{1,0:T(8,128)(2,1)S(1)} %copy-done.4, ...), custom_call_target="tpu_custom_call" | custom-call | flops 536870912 | bytes 5242880 | tf_op jit(solution)/shard_map/device_states/pallas_call | solution.py:131
  9.9 1.3 %collective-permute-start = (f32[136,256]{1,0:T(8,128)S(1)}, f32[136,256]{1,0:T(8,128)S(1)}, u32[]{:S(2)}, u32[]{:S(2)}) collective-permute-start(f32[136,256]{1,0:T(8,128)S(1)} %get-tuple-element.24), channel_id=1, source_target_pairs={{0,4},{4,8},{1,5},{5,9},{2,6},{6,10},{3,7},{7,11},{16,20},{20,24},... | collective-permute-start | bytes 417800 | tf_op jit(solution)/shard_map/ppermute | solution.py:417
  11.2 4.6 %collective-permute-start.1 = (f32[136,256]{1,0:T(8,128)S(1)}, f32[136,256]{1,0:T(8,128)S(1)}, u32[]{:S(2)}, u32[]{:S(2)}) collective-permute-start(f32[136,256]{1,0:T(8,128)S(1)} %get-tuple-element.25), channel_id=1, source_target_pairs={{8,4},{0,8},{9,5},{1,9},{10,6},{2,10},{11,7},{3,11},{24,20},{16,24... | collective-permute-start | bytes 417800 | tf_op jit(solution)/shard_map/ppermute | solution.py:418
  15.8 0.0 copy-done.5
  15.8 0.0 copy-done
  15.8 0.0 copy-done.2
  15.8 7.0 %local_part.2 = (bf16[2048,512]{1,0:T(8,128)(2,1)S(1)}, bf16[2048,512]{1,0:T(8,128)(2,1)S(1)}, bf16[2048,128]{1,0:T(8,128)(2,1)S(1)}, f32[1,512]{1,0:T(1,128)}, f32[128,512]{1,0:T(8,128)S(1)}) custom-call(f32[8,4096]{1,0:T(8,128)S(1)} %copy-done.3, bf16[4096,128]{1,0:T(8,128)(2,1)S(1)} %copy-done.2, bf16[4096,512]{1,0:T(8,128)(2,1)S(1)} %copy-done, ...), custom_call_target="tpu_custom_call" | custom-call | flops 1073741824 | bytes 9437184 | tf_op jit(solution)/shard_map/local_part/pallas_call | solution.py:234
  22.8 0.0 collective-permute-done.one_ref
  22.9 0.0 collective-permute-done.1.two_ref
  22.9 1.9 %collective-permute-start.2 = (f32[128,256]{1,0:T(8,128)S(1)}, f32[128,256]{1,0:T(8,128)S(1)}, u32[]{:S(2)}, u32[]{:S(2)}) collective-permute-start(f32[128,256]{1,0:T(8,128)S(1)} %get-tuple-element.32), channel_id=1, source_target_pairs={{4,8},{8,12},{5,9},{9,13},{6,10},{10,14},{7,11},{11,15},{20,24},{2... | collective-permute-start | bytes 393224 | tf_op jit(solution)/shard_map/ppermute | solution.py:423
  24.8 4.1 %collective-permute-start.3 = (f32[128,256]{1,0:T(8,128)S(1)}, f32[128,256]{1,0:T(8,128)S(1)}, u32[]{:S(2)}, u32[]{:S(2)}) collective-permute-start(f32[128,256]{1,0:T(8,128)S(1)} %get-tuple-element.33), channel_id=1, source_target_pairs={{4,12},{8,4},{5,13},{9,5},{6,14},{10,6},{7,15},{11,7},{20,28},{24,... | collective-permute-start | bytes 393224 | tf_op jit(solution)/shard_map/ppermute | solution.py:424
  29.0 7.1 %local_part.3 = (bf16[2048,512]{1,0:T(8,128)(2,1)S(1)}, bf16[2048,512]{1,0:T(8,128)(2,1)S(1)}, bf16[2048,128]{1,0:T(8,128)(2,1)S(1)}, f32[1,512]{1,0:T(1,128)S(1)}, f32[128,512]{1,0:T(8,128)}) custom-call(f32[8,4096]{1,0:T(8,128)S(1)} %copy-done.3, bf16[4096,128]{1,0:T(8,128)(2,1)S(1)} %copy-done.2, bf16[4096,512]{1,0:T(8,128)(2,1)S(1)} %copy-done, ...), custom_call_target="tpu_custom_call" | custom-call | flops 1073741824 | bytes 9437184 | tf_op jit(solution)/shard_map/local_part/pallas_call | solution.py:234
  36.1 0.0 collective-permute-done.2.rest_0_
  36.1 0.0 collective-permute-done.3.rest_1_
  36.1 4.2 %final_part.1 = bf16[4096,512]{1,0:T(8,128)(2,1)} custom-call(s32[1]{0:T(128)} %bitcast.place_ref, f32[128,256]{1,0:T(8,128)S(1)} %collective-permute-done.2.rest_0_, f32[128,256]{1,0:T(8,128)S(1)} %collective-permute-done.3.rest_1_, f32[128,256]{1,0:T(8,128)S(1)} %get-tuple-element.34.rest_2_, bf16[2048,128]{1,0:T(8,128)(2,1)S(1)} %get-tuple-element.35.rest_3_, ...), custom_call_target="tpu_custom_call" | custom-call | flops 1073741824 | bytes 13631488 | tf_op jit(solution)/shard_map/final_part/pallas_call | solution.py:323
  (2 shorter events, 0.0 us)
Async XLA Ops:
  0.0 15.8 %copy-start.5 = (f32[512]{0:T(512)S(1)}, f32[512]{0:T(512)}, u32[]{:S(2)}) copy-start(f32[512]{0:T(512)} %param.11) | copy-start | bytes 6148
  0.0 15.8 %copy-start = (bf16[4096,512]{1,0:T(8,128)(2,1)S(1)}, bf16[4096,512]{1,0:T(8,128)(2,1)}, u32[]{:S(2)}) copy-start(bf16[4096,512]{1,0:T(8,128)(2,1)} %gate_hbm.3) | copy-start | bytes 12582916
  0.0 2.3 %copy-start.1 = (bf16[4096,512]{1,0:T(8,128)(2,1)S(1)}, bf16[4096,512]{1,0:T(8,128)(2,1)}, u32[]{:S(2)}) copy-start(bf16[4096,512]{1,0:T(8,128)(2,1)} %signal_hbm.1) | copy-start | bytes 12582916
  2.3 1.1 %copy-start.3 = (f32[8,4096]{1,0:T(8,128)S(1)}, f32[8,4096]{1,0:T(8,128)}, u32[]{:S(2)}) copy-start(f32[8,4096]{1,0:T(8,128)} %decay_hbm.5) | copy-start | bytes 393220
  3.4 1.2 %copy-start.4 = (bf16[4096,128]{1,0:T(8,128)(2,1)S(1)}, bf16[4096,128]{1,0:T(8,128)(2,1)}, u32[]{:S(2)}) copy-start(bf16[4096,128]{1,0:T(8,128)(2,1)} %entry_hbm.1) | copy-start | bytes 3145732
  4.7 11.1 %copy-start.2 = (bf16[4096,128]{1,0:T(8,128)(2,1)S(1)}, bf16[4096,128]{1,0:T(8,128)(2,1)}, u32[]{:S(2)}) copy-start(bf16[4096,128]{1,0:T(8,128)(2,1)} %readout_hbm.3) | copy-start | bytes 3145732
  9.9 12.9 %collective-permute-start = (f32[136,256]{1,0:T(8,128)S(1)}, f32[136,256]{1,0:T(8,128)S(1)}, u32[]{:S(2)}, u32[]{:S(2)}) collective-permute-start(f32[136,256]{1,0:T(8,128)S(1)} %get-tuple-element.24), channel_id=1, source_target_pairs={{0,4},{4,8},{1,5},{5,9},{2,6},{6,10},{3,7},{7,11},{16,20},{20,24},... | collective-permute-start | bytes 417800 | tf_op jit(solution)/shard_map/ppermute | solution.py:417
  11.2 11.6 %collective-permute-start.1 = (f32[136,256]{1,0:T(8,128)S(1)}, f32[136,256]{1,0:T(8,128)S(1)}, u32[]{:S(2)}, u32[]{:S(2)}) collective-permute-start(f32[136,256]{1,0:T(8,128)S(1)} %get-tuple-element.25), channel_id=1, source_target_pairs={{8,4},{0,8},{9,5},{1,9},{10,6},{2,10},{11,7},{3,11},{24,20},{16,24... | collective-permute-start | bytes 417800 | tf_op jit(solution)/shard_map/ppermute | solution.py:418
  22.9 13.2 %collective-permute-start.2 = (f32[128,256]{1,0:T(8,128)S(1)}, f32[128,256]{1,0:T(8,128)S(1)}, u32[]{:S(2)}, u32[]{:S(2)}) collective-permute-start(f32[128,256]{1,0:T(8,128)S(1)} %get-tuple-element.32), channel_id=1, source_target_pairs={{4,8},{8,12},{5,9},{9,13},{6,10},{10,14},{7,11},{11,15},{20,24},{2... | collective-permute-start | bytes 393224 | tf_op jit(solution)/shard_map/ppermute | solution.py:423
  24.8 11.3 %collective-permute-start.3 = (f32[128,256]{1,0:T(8,128)S(1)}, f32[128,256]{1,0:T(8,128)S(1)}, u32[]{:S(2)}, u32[]{:S(2)}) collective-permute-start(f32[128,256]{1,0:T(8,128)S(1)} %get-tuple-element.33), channel_id=1, source_target_pairs={{4,12},{8,4},{5,13},{9,5},{6,14},{10,6},{7,15},{11,7},{20,28},{24,... | collective-permute-start | bytes 393224 | tf_op jit(solution)/shard_map/ppermute | solution.py:424

commit v3 on v2

v3 whole, which is shorter than its diff:
```python
import functools

import jax
import jax.numpy as jnp
from jax import lax
from jax.experimental import pallas as pl
from jax.experimental.pallas import tpu as pltpu
from jax.sharding import PartitionSpec as P

CHUNK = 128
HEAD_ROWS = 8
EPSILON = 1e-05
F32 = jnp.float32
BF16 = jnp.bfloat16
TN = (((0,), (0,)), ((), ()))
NT = (((1,), (1,)), ((), ()))
IN_HBM = pl.BlockSpec(memory_space=pltpu.HBM)
IN_VMEM = pl.BlockSpec(memory_space=pltpu.VMEM)


def mm(left, right, dims=(((1,), (0,)), ((), ()))):
    return lax.dot_general(left, right, dims, preferred_element_type=F32)


def two_terms(value):
    high = value.astype(BF16)
    return high, (value - high.astype(F32)).astype(BF16)


def spread_matrix(width, head_size):
    row = lax.broadcasted_iota(jnp.int32, (2 * HEAD_ROWS, width), 0)
    column = lax.broadcasted_iota(jnp.int32, (2 * HEAD_ROWS, width), 1)
    own = lax.rem(row, HEAD_ROWS) == lax.div(column, head_size)
    return own.astype(F32).astype(BF16)


def stacked(decay):
    chunks = decay.shape[1] // CHUNK
    return jnp.concatenate([decay[:, c * CHUNK : (c + 1) * CHUNK] for c in range(chunks)], axis=0)


def sums(decay_rows, matrix):
    high = decay_rows.astype(BF16)
    rest = decay_rows - high.astype(F32)
    middle = rest.astype(BF16)
    low = (rest - middle.astype(F32)).astype(BF16)
    return mm(high, matrix) + (mm(middle, matrix) + mm(low, matrix))


def pair_rows(value):
    high, low = two_terms(value)
    return jnp.concatenate([high, low], axis=0)


def indicator(test):
    return test.astype(F32).astype(BF16)


def spread_rows(factor_ref, chunks, spread):
    return jnp.concatenate([mm(factor_ref[c], spread, TN) for c in chunks], axis=0)


def copy_rows(source, target, semaphore, start, rows):
    where = pl.ds(start, rows)
    return pltpu.make_async_copy(source.at[where], target.at[where], semaphore)


def state_kernel(split, head_size, pieces, place_ref, decay_hbm, entry_hbm, signal_hbm, *rest):
    outs, (entry_ref, signal_ref, decay_ref, factor_ref, semaphores) = rest[:-5], rest[-5:]
    length, width = signal_ref.shape
    rows = length // pieces
    chunks = length // CHUNK
    decay_copy = pltpu.make_async_copy(decay_hbm, decay_ref, semaphores.at[2 * pieces])
    decay_copy.start()
    copies = []
    for k in range(pieces):
        copies.append(copy_rows(entry_hbm, entry_ref, semaphores.at[k], k * rows, rows))
        copies.append(copy_rows(signal_hbm, signal_ref, semaphores.at[pieces + k], k * rows, rows))
    for copy in copies:
        copy.start()
    spread = spread_matrix(width, head_size)
    decay_copy.wait()
    tall = stacked(decay_ref[...])
    s_from = lax.broadcasted_iota(jnp.int32, (CHUNK, 2 * CHUNK), 0)
    s_to = lax.broadcasted_iota(jnp.int32, (CHUNK, 2 * CHUNK), 1)
    both = sums(tall, indicator((s_from > s_to) | (s_to >= CHUNK)))
    later = jnp.zeros((HEAD_ROWS, CHUNK), F32)
    for c in reversed(range(chunks)):
        part = both[c * HEAD_ROWS : (c + 1) * HEAD_ROWS]
        factor_ref[c] = pair_rows(jnp.exp(part[:, :CHUNK] + later))
        later = later + part[:, CHUNK:]
    gain = mm(pair_rows(jnp.exp(later[:, :HEAD_ROWS])), spread, TN)
    states = None
    for k in range(pieces):
        copies[2 * k].wait()
        copies[2 * k + 1].wait()
        where = pl.ds(k * rows, rows)
        here = range(k * rows // CHUNK, (k + 1) * rows // CHUNK)
        scaled = (signal_ref[where, :].astype(F32) * spread_rows(factor_ref, here, spread)).astype(BF16)
        term = mm(entry_ref[where, :], scaled, TN)
        states = term if states is None else states + term
    size = states.shape[0]
    if split:
        own_ref, first_ref, second_ref = outs
        half = width // 2
        for k in range(2):
            own_ref[k, :size, :] = states[:, k * half : (k + 1) * half]
            own_ref[k, size:, :] = gain[:, k * half : (k + 1) * half]

        @pl.when(place_ref[0] == 0)
        def _():
            first_ref[...] = own_ref[0]
            second_ref[...] = own_ref[1]

        @pl.when(place_ref[0] != 0)
        def _():
            first_ref[...] = own_ref[1]
            second_ref[...] = own_ref[0]
    else:
        (own_ref,) = outs
        own_ref[:size, :] = states
        own_ref[size:, :] = gain


def local_states(place, decay, entry_map, signal, head_size, split, pieces):
    length, width = signal.shape
    state_size = entry_map.shape[1]
    tall = state_size + HEAD_ROWS
    if split:
        shapes = [(2, tall, width // 2), (tall, width // 2), (tall, width // 2)]
    else:
        shapes = [(tall, width)]
    return pl.pallas_call(
        functools.partial(state_kernel, split, head_size, pieces),
        in_specs=[pl.BlockSpec(memory_space=pltpu.SMEM)] + [IN_HBM] * 3,
        out_specs=[IN_VMEM] * (len(shapes) + 2),
        out_shape=[pltpu.VMEM(s, F32) for s in shapes]
        + [pltpu.VMEM((length, state_size), BF16), pltpu.VMEM((length, width), BF16)],
        scratch_shapes=[
            pltpu.VMEM((HEAD_ROWS, length), F32),
            pltpu.VMEM((length // CHUNK, 2 * HEAD_ROWS, CHUNK), BF16),
            pltpu.SemaphoreType.DMA((2 * pieces + 1,)),
        ],
        name="device_states",
        compiler_params=pltpu.CompilerParams(vmem_limit_bytes=56 << 20),
        cost_estimate=pl.CostEstimate(
            flops=2 * length * width * state_size,
            bytes_accessed=2 * length * (width + state_size),
            transcendentals=0,
        ),
    )(place, decay, entry_map, signal)


def by_head(value, factor):
    rows, width = value.shape
    return (value.reshape(rows // HEAD_ROWS, HEAD_ROWS, width) * factor[None]).reshape(rows, width)


def local_kernel(base, head_size, group, decay_ref, readout_ref, gate_ref, entry_ref, signal_ref, state_in, *rest):
    inside_ref, share_ref, state_ref, in_ref, out_ref = rest
    length, width = signal_ref.shape
    sides, part_rows, side = inside_ref.shape
    first = base // CHUNK
    many = part_rows // CHUNK
    spread = spread_matrix(width, head_size)
    tall = stacked(decay_ref[...])
    half = CHUNK // 2
    s_from = lax.broadcasted_iota(jnp.int32, (CHUNK, CHUNK), 0)
    s_to = lax.broadcasted_iota(jnp.int32, (CHUNK, CHUNK), 1)
    early = (s_from < half).astype(F32)
    centred = ((s_from <= s_to).astype(F32) - early).astype(BF16)
    matrix = jnp.concatenate([centred, early.astype(BF16), (1.0 - early).astype(BF16)], axis=1)
    three = sums(tall, matrix)
    before = jnp.zeros((HEAD_ROWS, HEAD_ROWS), F32)
    to_here, to_next = [], []
    for c in range(first + many):
        part = three[c * HEAD_ROWS : (c + 1) * HEAD_ROWS]
        to_middle = part[:, CHUNK : CHUNK + HEAD_ROWS]
        onward = part[:, 2 * CHUNK : 2 * CHUNK + HEAD_ROWS]
        if c >= first:
            from_middle = part[:, :CHUNK]
            in_ref[c - first] = pair_rows(jnp.exp(-from_middle))
            out_ref[c - first] = pair_rows(jnp.exp(from_middle))
            to_here.append(pair_rows(jnp.exp(before + to_middle)))
            if (c + 1) * CHUNK < length:
                following = three[(c + 1) * HEAD_ROWS : (c + 2) * HEAD_ROWS, CHUNK : CHUNK + HEAD_ROWS]
                to_next.append(pair_rows(jnp.exp(onward + following)))
            else:
                to_next.append(pair_rows(jnp.exp(onward)))
        before = before + (to_middle + onward)
    causal = s_from >= s_to
    state = state_in[...] if base else jnp.zeros(state_ref.shape, F32)
    for start in range(0, many, group):
        here = range(start, start + group)
        where = pl.ds(base + start * CHUNK, group * CHUNK)
        there = pl.ds(start * CHUNK, group * CHUNK)
        cut = lambda value, j: value[j * CHUNK : (j + 1) * CHUNK]
        entry = entry_ref[where, :]
        readout = readout_ref[where, :]
        scaled = (signal_ref[where, :].astype(F32) * spread_rows(in_ref, here, spread)).astype(BF16)
        scores, added, passed = [], [], []
        for j in range(group):
            products = mm(cut(readout, j), cut(entry, j), NT)
            scores.append(jnp.where(causal, products, 0.0).astype(BF16))
            added.append(mm(cut(entry, j), cut(scaled, j), TN))
        for j in range(group):
            passed.append(state.astype(BF16))
            state = by_head(state + added[j], mm(to_next[start + j], spread, TN))
        output = jnp.concatenate(
            [
                mm(
                    jnp.concatenate([scores[j], cut(readout, j)], axis=1),
                    jnp.concatenate([cut(scaled, j), passed[j]], axis=0),
                )
                for j in range(group)
            ],
            axis=0,
        )
        gate = gate_ref[where, :].astype(F32)
        opened = gate / (1.0 + jnp.exp(-gate)) * spread_rows(out_ref, here, spread)
        inside = (output * opened).astype(BF16)
        share = jnp.concatenate(
            [by_head(cut(opened, j), mm(to_here[start + j], spread, TN)) for j in range(group)], axis=0
        ).astype(BF16)
        for k in range(sides):
            inside_ref[k, there, :] = inside[:, k * side : (k + 1) * side]
            share_ref[k, there, :] = share[:, k * side : (k + 1) * side]
    state_ref[...] = state


def local_part(index, parts, decay, readout, gate_input, entry_map, signal, state, head_size, sides, group):
    length, width = signal.shape
    state_size = entry_map.shape[1]
    rows = length // parts
    return pl.pallas_call(
        functools.partial(local_kernel, index * rows, head_size, group),
        in_specs=[IN_VMEM] * 6,
        out_specs=[IN_VMEM] * 3,
        out_shape=[pltpu.VMEM((sides, rows, width // sides), BF16)] * 2 + [pltpu.VMEM((state_size, width), F32)],
        scratch_shapes=[pltpu.VMEM((rows // CHUNK, 2 * HEAD_ROWS, CHUNK), BF16)] * 2,
        name="local_part",
        compiler_params=pltpu.CompilerParams(vmem_limit_bytes=16 << 20),
        cost_estimate=pl.CostEstimate(
            flops=8 * length * width * state_size // parts,
            bytes_accessed=2 * length * (4 * width + 2 * state_size) // parts,
            transcendentals=length * width // parts,
        ),
    )(decay, readout, gate_input, entry_map, signal, state)


def final_kernel(turn, head_size, parts, rows, place_ref, *rest):
    count = 1 if turn is None else 2
    incoming, rest = rest[:count], rest[count:]
    readout_ref, gain_ref, *rest = rest
    groups, rest = [rest[2 * p : 2 * p + 2] for p in range(parts)], rest[2 * parts :]
    result_hbm, result_ref, terms_ref, semaphores = rest[-4:]
    size = readout_ref.shape[1]
    _, part_rows, width = groups[0][0].shape

    def keep(value):
        high, low = two_terms(value)
        terms_ref[:size, :] = high
        terms_ref[size:, :] = low

    if turn is None:
        side = 0
        keep(incoming[0][...])
    else:
        place = place_ref[0]
        side = jnp.where(place == 1, turn, 1 - turn)
        other = (place == 1) | (place == 2) if turn == 0 else place == 2

        @pl.when(other)
        def _():
            keep(incoming[0][...])

        @pl.when(jnp.logical_not(other))
        def _():
            keep(incoming[1][...])

    group = min(width, 256)
    row = lax.broadcasted_iota(jnp.int32, (group, group), 0)
    column = lax.broadcasted_iota(jnp.int32, (group, group), 1)
    same = lax.div(row, head_size) == lax.div(column, head_size)
    average = jnp.where(same, 1.0 / head_size, 0.0).astype(BF16)
    gain = gain_ref[side]
    terms = terms_ref[...]
    columns = pl.ds(0, width) if turn is None else pl.ds(pl.multiple_of(side * width, width), width)
    copies = []
    for p, (inside_ref, share_ref) in enumerate(groups):
        for start in range(0, part_rows, rows):
            where = pl.ds(start, rows)
            there = pl.ds(p * part_rows + start, rows)
            readout = readout_ref[there, :]
            across = mm(jnp.concatenate([readout, readout], axis=1), terms)
            gated = inside_ref[side, where, :].astype(F32) + share_ref[side, where, :].astype(F32) * across
            squares = (gated * gated).astype(BF16)
            mean = jnp.concatenate(
                [mm(squares[:, g : g + group], average) for g in range(0, width, group)], axis=1
            )
            result_ref[there, :] = (gated * lax.rsqrt(mean + EPSILON) * gain).astype(BF16)
            copy = pltpu.make_async_copy(
                result_ref.at[there], result_hbm.at[there, columns], semaphores.at[len(copies)]
            )
            copy.start()
            copies.append(copy)
    for copy in copies:
        copy.wait()


def final_part(turn, place, incoming, readout, norm_gain, groups, kept, head_size, rows):
    sides, part_rows, width = groups[0][0].shape
    length = part_rows * len(groups)
    state_size = readout.shape[1]
    arguments = [place, *incoming, readout, norm_gain, *[v for g in groups for v in g]]
    in_specs = [pl.BlockSpec(memory_space=pltpu.SMEM)] + [IN_VMEM] * (len(arguments) - 1)
    aliases = {}
    if kept is not None:
        aliases = {len(arguments): 0}
        arguments.append(kept)
        in_specs.append(IN_HBM)
    return pl.pallas_call(
        functools.partial(final_kernel, turn, head_size, len(groups), rows),
        in_specs=in_specs,
        out_specs=IN_HBM,
        out_shape=jax.ShapeDtypeStruct((length, width * sides), BF16),
        input_output_aliases=aliases,
        scratch_shapes=[
            pltpu.VMEM((length, width), BF16),
            pltpu.VMEM((2 * state_size, width), BF16),
            pltpu.SemaphoreType.DMA((length // rows,)),
        ],
        name="final_part",
        compiler_params=pltpu.CompilerParams(vmem_limit_bytes=16 << 20),
        cost_estimate=pl.CostEstimate(
            flops=4 * length * width * state_size,
            bytes_accessed=2 * length * (3 * width + state_size),
            transcendentals=length * width,
        ),
    )(*arguments)


def blend_kernel(place_ref, one_ref, two_ref, own_ref, first_ref, second_ref, kept_ref):
    size = kept_ref.shape[0]
    width = kept_ref.shape[1]

    def scaled(rows_ref, value):
        gain = rows_ref[size:, :]
        shape = (size // HEAD_ROWS, HEAD_ROWS, width)
        return (value.reshape(shape) * gain[None]).reshape(size, width)

    @pl.when(place_ref[0] == 1)
    def _():
        mine = own_ref.at[0]
        first = one_ref[:size, :]
        second = mine[:size, :] + scaled(mine, first)
        first_ref[...] = second
        second_ref[...] = two_ref[:size, :] + scaled(two_ref, second)
        kept_ref[...] = first

    @pl.when(place_ref[0] != 1)
    def _():
        mine = own_ref.at[1]
        first = two_ref[:size, :]
        second = one_ref[:size, :] + scaled(one_ref, first)
        first_ref[...] = mine[:size, :] + scaled(mine, second)
        second_ref[...] = first
        kept_ref[...] = second


def blend(place, one, two, own):
    size = one.shape[0] - HEAD_ROWS
    width = one.shape[1]
    return pl.pallas_call(
        blend_kernel,
        in_specs=[pl.BlockSpec(memory_space=pltpu.SMEM)] + [IN_VMEM] * 3,
        out_specs=[IN_VMEM] * 3,
        out_shape=[pltpu.VMEM((size, width), F32)] * 3,
        name="blend",
        compiler_params=pltpu.CompilerParams(vmem_limit_bytes=4 << 20),
    )(place, one, two, own)


def scan_devices(own, devices):
    size = own.shape[0] - HEAD_ROWS
    gain = lambda v: v[size : size + 1]
    reach, before = own, None
    shift = 1
    while shift < devices:
        came = lax.ppermute(reach, "tm", [(i, i + shift) for i in range(devices - shift)])
        join = lambda later: jnp.concatenate(
            [later[:size] + gain(later) * came[:size], later[size:] * came[size:]], axis=0
        )
        before = came if before is None else join(before)
        reach = join(reach)
        shift *= 2
    if before is None:
        return jnp.zeros_like(own[:size])
    return before[:size]


def shards(devices, signal, entry_map, readout, gate_input, log_decay, norm_gain):
    heads, length = log_decay.shape
    width = signal.shape[1]
    head_size = width // heads
    split = devices == 4 and width % 256 == 0
    sides = 2 if split else 1
    decay = log_decay
    if heads < HEAD_ROWS:
        decay = jnp.pad(log_decay, ((0, HEAD_ROWS - heads), (0, 0)))
    place = lax.axis_index("tm").astype(jnp.int32).reshape(1)
    *made, entry_map, signal = local_states(place, decay, entry_map, signal, head_size, split, 4)
    common = (decay, readout, gate_input, entry_map, signal)
    nothing = jnp.zeros((8, 128), F32)
    if split:
        own, first, second = made
        one = lax.ppermute(first, "tm", [(0, 1), (1, 2)])
        two = lax.ppermute(second, "tm", [(2, 1), (0, 2)])
    *before, state = local_part(0, 2, *common, nothing, head_size, sides, 4)
    if split:
        one, two, state = lax.optimization_barrier((one, two, state))
        first, second, kept = blend(place, one, two, own)
        one = lax.ppermute(first, "tm", [(1, 2), (2, 3)])
        two = lax.ppermute(second, "tm", [(1, 3), (2, 1)])
    else:
        total = scan_devices(made[0], devices)
    *after, _ = local_part(1, 2, *common, state, head_size, sides, 4)
    common = (readout, norm_gain.reshape(sides, 1, width // sides), (before, after))
    if split:
        result = final_part(0, place, (kept, one), *common, None, head_size, 1024)
        return final_part(1, place, (one, two), *common, result, head_size, 1024)
    return final_part(None, place, (total,), *common, None, head_size, 1024)


def solution(mesh):
    in_specs = (
        P(("parts", "tm"), ("head", "sub")),
        P(("parts", "tm"), None),
        P(("parts", "tm"), None),
        P(("parts", "tm"), ("head", "sub")),
        P(("head", "sub"), ("parts", "tm")),
        P(("head", "sub")),
    )
    out_specs = P(("parts", "tm"), ("head", "sub"))
    body = functools.partial(shards, mesh.shape["tm"])
    return jax.shard_map(body, mesh=mesh, in_specs=in_specs, out_specs=out_specs, check_vma=False)
```

time: 40.7 us -> 32.6 us (0.80)
  the two profiles are of different devices: /device:TPU:18 before, /device:TPU:20 now
where the time goes in v3:
time: 32.6 us; the launch traced here: 32.4 us
  Pallas kernels  18.2 us (56%)
  starting transfers between devices  11.7 us (36%)
  local copies, waits for them, and re-layouts  2.2 us (7%)
    pallas_call x2, Pallas kernels, local_part(): pl.pallas_call(functools.partial(local_kernel, index * rows, head_size, g...  9.02 us
    pallas_call x2, Pallas kernels, final_part(): pl.pallas_call(functools.partial(final_kernel, turn, head_size, len(group...  5.13 us
    ppermute x1, starting transfers between devices, shards(): two = lax.ppermute(second, 'tm', [(2, 1), (0, 2)])  4.55 us
    pallas_call x1, Pallas kernels, local_states(): pl.pallas_call(functools.partial(state_kernel, split, head_size, pieces),...  4 us
    ppermute x1, starting transfers between devices, shards(): two = lax.ppermute(second, 'tm', [(1, 3), (2, 1)])  3.93 us
    unnamed x8, local copies, waits for them, and re-layouts  2.2 us
    ppermute x1, starting transfers between devices, shards(): one = lax.ppermute(first, 'tm', [(1, 2), (2, 3)])  1.92 us
    ppermute x1, starting transfers between devices, shards(): one = lax.ppermute(first, 'tm', [(0, 1), (1, 2)])  1.29 us
  transfers between devices with their start and end apart: 4, of which 0 were waited for; matrix products, arithmetic and copies ran while one was open for 0% of the time, Pallas kernels for 36%

profile of v3, /device:TPU:20, one launch (start us, length us, event | category | flops | bytes accessed | tf_op | source)
XLA Modules:
  0.0 32.4 jit_solution(2866864651929103933)
XLA Ops:
  0.0 0.0 copy-start.2
  0.0 0.0 copy-start.1
  0.0 4.0 %device_states.1 = (f32[2,136,256]{2,1,0:T(8,128)S(1)}, f32[136,256]{1,0:T(8,128)S(1)}, f32[136,256]{1,0:T(8,128)S(1)}, bf16[4096,128]{1,0:T(8,128)(2,1)S(1)}, bf16[4096,512]{1,0:T(8,128)(2,1)S(1)}) custom-call(s32[1]{0:T(128)} %bitcast.place_ref, f32[8,4096]{1,0:T(8,128)} %decay_ref.3, bf16[4096,128]{1,0:T(8,128)(2,1)} %entry_hbm.1, ...), custom_call_target="tpu_custom_call" | custom-call | flops 536870912 | bytes 5242880 | tf_op jit(solution)/shard_map/device_states/pallas_call | solution.py:133
  4.0 1.3 %collective-permute-start = (f32[136,256]{1,0:T(8,128)S(1)}, f32[136,256]{1,0:T(8,128)S(1)}, u32[]{:S(2)}, u32[]{:S(2)}) collective-permute-start(f32[136,256]{1,0:T(8,128)S(1)} %get-tuple-element.21), channel_id=1, source_target_pairs={{0,4},{4,8},{1,5},{5,9},{2,6},{6,10},{3,7},{7,11},{16,20},{20,24},... | collective-permute-start | bytes 417800 | tf_op jit(solution)/shard_map/ppermute | solution.py:417
  5.3 4.6 %collective-permute-start.1 = (f32[136,256]{1,0:T(8,128)S(1)}, f32[136,256]{1,0:T(8,128)S(1)}, u32[]{:S(2)}, u32[]{:S(2)}) collective-permute-start(f32[136,256]{1,0:T(8,128)S(1)} %get-tuple-element.22), channel_id=1, source_target_pairs={{8,4},{0,8},{9,5},{1,9},{10,6},{2,10},{11,7},{3,11},{24,20},{16,24... | collective-permute-start | bytes 417800 | tf_op jit(solution)/shard_map/ppermute | solution.py:418
  9.9 0.0 copy-done.2
  9.9 0.0 copy-done.1
  9.9 0.0 copy-start
  9.9 2.2 %copy-done = bf16[4096,512]{1,0:T(8,128)(2,1)S(1)} copy-done((bf16[4096,512]{1,0:T(8,128)(2,1)S(1)}, bf16[4096,512]{1,0:T(8,128)(2,1)}, u32[]{:S(2)}) %copy-start) | copy-done | bytes 4194328
  12.1 4.4 %local_part.2 = (bf16[2,2048,256]{2,1,0:T(8,128)(2,1)S(1)}, bf16[2,2048,256]{2,1,0:T(8,128)(2,1)S(1)}, f32[128,512]{1,0:T(8,128)S(1)}) custom-call(f32[8,4096]{1,0:T(8,128)S(1)} %copy-done.2, bf16[4096,128]{1,0:T(8,128)(2,1)S(1)} %copy-done.1, bf16[4096,512]{1,0:T(8,128)(2,1)S(1)} %copy-done, bf16[4096,128]{1,0:T(8,128)(2,1)S(1)} %get-tuple-element.23.entry_ref, ...), custom_call_target="tpu_custom_call" | custom-call | flops 1073741824 | bytes 9437184 | tf_op jit(solution)/shard_map/local_part/pallas_call | solution.py:235
  16.5 0.0 collective-permute-done.one_ref
  16.5 0.0 collective-permute-done.1.two_ref
  16.5 0.1 blend.1
  16.6 1.9 %collective-permute-start.2 = (f32[128,256]{1,0:T(8,128)S(1)}, f32[128,256]{1,0:T(8,128)S(1)}, u32[]{:S(2)}, u32[]{:S(2)}) collective-permute-start(f32[128,256]{1,0:T(8,128)S(1)} %get-tuple-element.29), channel_id=1, source_target_pairs={{4,8},{8,12},{5,9},{9,13},{6,10},{10,14},{7,11},{11,15},{20,24},{2... | collective-permute-start | bytes 393224 | tf_op jit(solution)/shard_map/ppermute | solution.py:423
  18.5 0.0 copy-start.3
  18.5 3.9 %collective-permute-start.3 = (f32[128,256]{1,0:T(8,128)S(1)}, f32[128,256]{1,0:T(8,128)S(1)}, u32[]{:S(2)}, u32[]{:S(2)}) collective-permute-start(f32[128,256]{1,0:T(8,128)S(1)} %get-tuple-element.30), channel_id=1, source_target_pairs={{4,12},{8,4},{5,13},{9,5},{6,14},{10,6},{7,15},{11,7},{20,28},{24,... | collective-permute-start | bytes 393224 | tf_op jit(solution)/shard_map/ppermute | solution.py:424
  22.5 4.6 %local_part.3 = (bf16[2,2048,256]{2,1,0:T(8,128)(2,1)S(1)}, bf16[2,2048,256]{2,1,0:T(8,128)(2,1)S(1)}, f32[128,512]{1,0:T(8,128)}) custom-call(f32[8,4096]{1,0:T(8,128)S(1)} %copy-done.2, bf16[4096,128]{1,0:T(8,128)(2,1)S(1)} %copy-done.1, bf16[4096,512]{1,0:T(8,128)(2,1)S(1)} %copy-done, bf16[4096,128]{1,0:T(8,128)(2,1)S(1)} %get-tuple-element.23.entry_ref, ...), custom_call_target="tpu_custom_call" | custom-call | flops 1073741824 | bytes 9437184 | tf_op jit(solution)/shard_map/local_part/pallas_call | solution.py:235
  27.1 0.0 collective-permute-done.2.rest_1_.rest_0_
  27.1 0.0 copy-done.3
  27.1 2.6 %final_part.2.rest_8_ = bf16[4096,512]{1,0:T(8,128)(2,1)} custom-call(s32[1]{0:T(128)} %bitcast.place_ref, f32[128,256]{1,0:T(8,128)S(1)} %get-tuple-element.36.rest_0_, f32[128,256]{1,0:T(8,128)S(1)} %collective-permute-done.2.rest_1_.rest_0_, bf16[4096,128]{1,0:T(8,128)(2,1)S(1)} %copy-done.1, f32[2,1,256]{2,1,0:T(1,128)S(1)} %bitcast.2, ...), custom_call_target="tpu_custom_call" | custom-call | flops 536870912 | bytes 7340032 | tf_op jit(solution)/shard_map/final_part/pallas_call | solution.py:322
  29.7 0.0 collective-permute-done.3.rest_1_
  29.7 2.5 %final_part.3 = bf16[4096,512]{1,0:T(8,128)(2,1)} custom-call(s32[1]{0:T(128)} %bitcast.place_ref, f32[128,256]{1,0:T(8,128)S(1)} %collective-permute-done.2.rest_1_.rest_0_, f32[128,256]{1,0:T(8,128)S(1)} %collective-permute-done.3.rest_1_, bf16[4096,128]{1,0:T(8,128)(2,1)S(1)} %copy-done.1, ...), custom_call_target="tpu_custom_call", output_to_operand_aliasing={{}: (9, {})} | custom-call | flops 536870912 | bytes 7340032 | tf_op jit(solution)/shard_map/final_part/pallas_call | solution.py:322
  (1 shorter events, 0.0 us)
Async XLA Ops:
  0.0 9.9 %copy-start.2 = (f32[8,4096]{1,0:T(8,128)S(1)}, f32[8,4096]{1,0:T(8,128)}, u32[]{:S(2)}) copy-start(f32[8,4096]{1,0:T(8,128)} %decay_ref.3) | copy-start | bytes 393220
  0.0 9.9 %copy-start.1 = (bf16[4096,128]{1,0:T(8,128)(2,1)S(1)}, bf16[4096,128]{1,0:T(8,128)(2,1)}, u32[]{:S(2)}) copy-start(bf16[4096,128]{1,0:T(8,128)(2,1)} %rest_2_.3) | copy-start | bytes 3145732
  4.0 12.5 %collective-permute-start = (f32[136,256]{1,0:T(8,128)S(1)}, f32[136,256]{1,0:T(8,128)S(1)}, u32[]{:S(2)}, u32[]{:S(2)}) collective-permute-start(f32[136,256]{1,0:T(8,128)S(1)} %get-tuple-element.21), channel_id=1, source_target_pairs={{0,4},{4,8},{1,5},{5,9},{2,6},{6,10},{3,7},{7,11},{16,20},{20,24},... | collective-permute-start | bytes 417800 | tf_op jit(solution)/shard_map/ppermute | solution.py:417
  5.3 11.2 %collective-permute-start.1 = (f32[136,256]{1,0:T(8,128)S(1)}, f32[136,256]{1,0:T(8,128)S(1)}, u32[]{:S(2)}, u32[]{:S(2)}) collective-permute-start(f32[136,256]{1,0:T(8,128)S(1)} %get-tuple-element.22), channel_id=1, source_target_pairs={{8,4},{0,8},{9,5},{1,9},{10,6},{2,10},{11,7},{3,11},{24,20},{16,24... | collective-permute-start | bytes 417800 | tf_op jit(solution)/shard_map/ppermute | solution.py:418
  9.9 2.2 %copy-start = (bf16[4096,512]{1,0:T(8,128)(2,1)S(1)}, bf16[4096,512]{1,0:T(8,128)(2,1)}, u32[]{:S(2)}) copy-start(bf16[4096,512]{1,0:T(8,128)(2,1)} %gate_ref.3) | copy-start | bytes 12582916
  16.6 10.5 %collective-permute-start.2 = (f32[128,256]{1,0:T(8,128)S(1)}, f32[128,256]{1,0:T(8,128)S(1)}, u32[]{:S(2)}, u32[]{:S(2)}) collective-permute-start(f32[128,256]{1,0:T(8,128)S(1)} %get-tuple-element.29), channel_id=1, source_target_pairs={{4,8},{8,12},{5,9},{9,13},{6,10},{10,14},{7,11},{11,15},{20,24},{2... | collective-permute-start | bytes 393224 | tf_op jit(solution)/shard_map/ppermute | solution.py:423
  18.5 8.5 %copy-start.3 = (f32[512]{0:T(512)S(1)}, f32[512]{0:T(512)}, u32[]{:S(2)}) copy-start(f32[512]{0:T(512)} %param.11) | copy-start | bytes 6148
  18.5 11.2 %collective-permute-start.3 = (f32[128,256]{1,0:T(8,128)S(1)}, f32[128,256]{1,0:T(8,128)S(1)}, u32[]{:S(2)}, u32[]{:S(2)}) collective-permute-start(f32[128,256]{1,0:T(8,128)S(1)} %get-tuple-element.30), channel_id=1, source_target_pairs={{4,12},{8,4},{5,13},{9,5},{6,14},{10,6},{7,15},{11,7},{20,28},{24,... | collective-permute-start | bytes 393224 | tf_op jit(solution)/shard_map/ppermute | solution.py:424

commit v4 on v3

--- a/solution.py
+++ b/solution.py
@@ -65,8 +65,8 @@
     return pltpu.make_async_copy(source.at[where], target.at[where], semaphore)
 
 
-def state_kernel(split, head_size, pieces, place_ref, decay_hbm, entry_hbm, signal_hbm, *rest):
-    outs, (entry_ref, signal_ref, decay_ref, factor_ref, semaphores) = rest[:-5], rest[-5:]
+def state_kernel(split, head_size, pieces, place_ref, decay_hbm, entry_hbm, signal_hbm, gate_hbm, *rest):
+    outs, (entry_ref, signal_ref, gate_ref, decay_ref, factor_ref, semaphores) = rest[:-6], rest[-6:]
     length, width = signal_ref.shape
     rows = length // pieces
     chunks = length // CHUNK
@@ -78,6 +78,10 @@
         copies.append(copy_rows(signal_hbm, signal_ref, semaphores.at[pieces + k], k * rows, rows))
     for copy in copies:
         copy.start()
+    gate_copy = pltpu.make_async_copy(
+        gate_hbm.at[pl.ds(0, gate_ref.shape[0])], gate_ref, semaphores.at[2 * pieces + 1]
+    )
+    gate_copy.start()
     spread = spread_matrix(width, head_size)
     decay_copy.wait()
     tall = stacked(decay_ref[...])
@@ -120,9 +124,10 @@
         (own_ref,) = outs
         own_ref[:size, :] = states
         own_ref[size:, :] = gain
-
-
-def local_states(place, decay, entry_map, signal, head_size, split, pieces):
+    gate_copy.wait()
+
+
+def local_states(place, decay, entry_map, signal, gate_input, head_size, split, pieces, parts):
     length, width = signal.shape
     state_size = entry_map.shape[1]
     tall = state_size + HEAD_ROWS
@@ -132,23 +137,27 @@
         shapes = [(tall, width)]
     return pl.pallas_call(
         functools.partial(state_kernel, split, head_size, pieces),
-        in_specs=[pl.BlockSpec(memory_space=pltpu.SMEM)] + [IN_HBM] * 3,
-        out_specs=[IN_VMEM] * (len(shapes) + 2),
+        in_specs=[pl.BlockSpec(memory_space=pltpu.SMEM)] + [IN_HBM] * 4,
+        out_specs=[IN_VMEM] * (len(shapes) + 3),
         out_shape=[pltpu.VMEM(s, F32) for s in shapes]
-        + [pltpu.VMEM((length, state_size), BF16), pltpu.VMEM((length, width), BF16)],
+        + [
+            pltpu.VMEM((length, state_size), BF16),
+            pltpu.VMEM((length, width), BF16),
+            pltpu.VMEM((length // parts, width), BF16),
+        ],
         scratch_shapes=[
             pltpu.VMEM((HEAD_ROWS, length), F32),
             pltpu.VMEM((length // CHUNK, 2 * HEAD_ROWS, CHUNK), BF16),
-            pltpu.SemaphoreType.DMA((2 * pieces + 1,)),
+            pltpu.SemaphoreType.DMA((2 * pieces + 2,)),
         ],
         name="device_states",
-        compiler_params=pltpu.CompilerParams(vmem_limit_bytes=56 << 20),
+        compiler_params=pltpu.CompilerParams(vmem_limit_bytes=52 << 20),
         cost_estimate=pl.CostEstimate(
             flops=2 * length * width * state_size,
             bytes_accessed=2 * length * (width + state_size),
             transcendentals=0,
         ),
-    )(place, decay, entry_map, signal)
+    )(place, decay, entry_map, signal, gate_input)
 
 
 def by_head(value, factor):
@@ -216,7 +225,7 @@
             ],
             axis=0,
         )
-        gate = gate_ref[where, :].astype(F32)
+        gate = gate_ref[there if gate_ref.shape[0] == part_rows else where, :].astype(F32)
         opened = gate / (1.0 + jnp.exp(-gate)) * spread_rows(out_ref, here, spread)
         inside = (output * opened).astype(BF16)
         share = jnp.concatenate(
@@ -268,7 +277,7 @@
     else:
         place = place_ref[0]
         side = jnp.where(place == 1, turn, 1 - turn)
-        other = (place == 1) | (place == 2) if turn == 0 else place == 2
+        other = (place == 1) | (place == 2)
 
         @pl.when(other)
         def _():
@@ -363,9 +372,16 @@
         mine = own_ref.at[1]
         first = two_ref[:size, :]
         second = one_ref[:size, :] + scaled(one_ref, first)
-        first_ref[...] = mine[:size, :] + scaled(mine, second)
-        second_ref[...] = first
+        second_ref[...] = second
         kept_ref[...] = second
+
+        @pl.when(place_ref[0] == 0)
+        def _():
+            first_ref[...] = mine[:size, :]
+
+        @pl.when(place_ref[0] != 0)
+        def _():
+            first_ref[...] = mine[:size, :] + scaled(mine, second)
 
 
 def blend(place, one, two, own):
@@ -409,22 +425,24 @@
     if heads < HEAD_ROWS:
         decay = jnp.pad(log_decay, ((0, HEAD_ROWS - heads), (0, 0)))
     place = lax.axis_index("tm").astype(jnp.int32).reshape(1)
-    *made, entry_map, signal = local_states(place, decay, entry_map, signal, head_size, split, 4)
-    common = (decay, readout, gate_input, entry_map, signal)
+    *made, entry_map, signal, gate_first = local_states(
+        place, decay, entry_map, signal, gate_input, head_size, split, 4, 2
+    )
+    common = (entry_map, signal)
     nothing = jnp.zeros((8, 128), F32)
     if split:
         own, first, second = made
         one = lax.ppermute(first, "tm", [(0, 1), (1, 2)])
         two = lax.ppermute(second, "tm", [(2, 1), (0, 2)])
-    *before, state = local_part(0, 2, *common, nothing, head_size, sides, 4)
+    *before, state = local_part(0, 2, decay, readout, gate_first, *common, nothing, head_size, sides, 4)
     if split:
         one, two, state = lax.optimization_barrier((one, two, state))
         first, second, kept = blend(place, one, two, own)
-        one = lax.ppermute(first, "tm", [(1, 2), (2, 3)])
-        two = lax.ppermute(second, "tm", [(1, 3), (2, 1)])
+        one = lax.ppermute(first, "tm", [(0, 1), (1, 2), (2, 3)])
+        two = lax.ppermute(second, "tm", [(1, 3)])
     else:
         total = scan_devices(made[0], devices)
-    *after, _ = local_part(1, 2, *common, state, head_size, sides, 4)
+    *after, _ = local_part(1, 2, decay, readout, gate_input, *common, state, head_size, sides, 4)
     common = (readout, norm_gain.reshape(sides, 1, width // sides), (before, after))
     if split:
         result = final_part(0, place, (kept, one), *common, None, head_size, 1024)

time: 32.6 us -> 30.3 us (0.929)
  the two profiles are of different devices: /device:TPU:20 before, /device:TPU:0 now
where the time goes in v4:
time: 30.3 us; the launch traced here: 30.1 us
  Pallas kernels  18.2 us (60%)
  starting transfers between devices  11.6 us (38%)
    pallas_call x2, Pallas kernels, local_part(): pl.pallas_call(functools.partial(local_kernel, index * rows, head_size, g...  9.02 us
    pallas_call x2, Pallas kernels, final_part(): pl.pallas_call(functools.partial(final_kernel, turn, head_size, len(group...  5.13 us
    ppermute x1, starting transfers between devices, shards(): one = lax.ppermute(first, 'tm', [(0, 1), (1, 2)])  4.93 us
    pallas_call x1, Pallas kernels, local_states(): pl.pallas_call(functools.partial(state_kernel, split, head_size, pieces),...  4.01 us
    ppermute x1, starting transfers between devices, shards(): one = lax.ppermute(first, 'tm', [(0, 1), (1, 2), (2, 3)])  3.69 us
    ppermute x1, starting transfers between devices, shards(): two = lax.ppermute(second, 'tm', [(2, 1), (0, 2)])  2.31 us
    ppermute x1, starting transfers between devices, shards(): two = lax.ppermute(second, 'tm', [(1, 3)])  0.67 us
  transfers between devices with their start and end apart: 4, of which 0 were waited for; matrix products, arithmetic and copies ran while one was open for 0% of the time, Pallas kernels for 39%

profile of v4, /device:TPU:0, one launch (start us, length us, event | category | flops | bytes accessed | tf_op | source)
XLA Modules:
  0.0 30.1 jit_solution(4068922033481330935)
XLA Ops:
  0.0 0.0 copy-start.1
  0.0 0.0 copy-start.2
  0.0 4.0 %device_states.1 = (f32[2,136,256]{2,1,0:T(8,128)S(1)}, f32[136,256]{1,0:T(8,128)S(1)}, f32[136,256]{1,0:T(8,128)S(1)}, bf16[4096,128]{1,0:T(8,128)(2,1)S(1)}, b...) custom-call(s32[1]{0:T(128)} %bitcast.place_ref, f32[8,4096]{1,0:T(8,128)} %decay_ref.3, ...), custom_call_target="tpu_custom_call" | custom-call | flops 536870912 | bytes 5242880 | tf_op jit(solution)/shard_map/device_states/pallas_call | solution.py:138
  4.0 4.9 %collective-permute-start = (f32[136,256]{1,0:T(8,128)S(1)}, f32[136,256]{1,0:T(8,128)S(1)}, u32[]{:S(2)}, u32[]{:S(2)}) collective-permute-start(f32[136,256]{1,0:T(8,128)S(1)} %get-tuple-element.22), channel_id=1, source_target_pairs={{0,4},{4,8},{1,5},{5,9},{2,6},{6,10},{3,7},{7,11},{16,20},{20,24},... | collective-permute-start | bytes 417800 | tf_op jit(solution)/shard_map/ppermute | solution.py:435
  9.0 2.3 %collective-permute-start.1 = (f32[136,256]{1,0:T(8,128)S(1)}, f32[136,256]{1,0:T(8,128)S(1)}, u32[]{:S(2)}, u32[]{:S(2)}) collective-permute-start(f32[136,256]{1,0:T(8,128)S(1)} %get-tuple-element.23), channel_id=1, source_target_pairs={{8,4},{0,8},{9,5},{1,9},{10,6},{2,10},{11,7},{3,11},{24,20},{16,24... | collective-permute-start | bytes 417800 | tf_op jit(solution)/shard_map/ppermute | solution.py:436
  11.3 0.0 copy-done.1
  11.3 0.0 copy-done.2
  11.3 0.0 copy-start
  11.3 4.4 %local_part.2 = (bf16[2,2048,256]{2,1,0:T(8,128)(2,1)S(1)}, bf16[2,2048,256]{2,1,0:T(8,128)(2,1)S(1)}, f32[128,512]{1,0:T(8,128)S(1)}) custom-call(f32[8,4096]{1,0:T(8,128)S(1)} %copy-done.2, bf16[4096,128]{1,0:T(8,128)(2,1)S(1)} %copy-done.1, bf16[2048,512]{1,0:T(8,128)(2,1)S(1)} %get-tuple-element.24.gate_ref, ...), custom_call_target="tpu_custom_call" | custom-call | flops 1073741824 | bytes 9437184 | tf_op jit(solution)/shard_map/local_part/pallas_call | solution.py:244
  15.7 0.0 collective-permute-done.one_ref
  15.8 0.0 collective-permute-done.1.two_ref
  15.8 0.1 blend.1
  15.8 3.7 %collective-permute-start.2 = (f32[128,256]{1,0:T(8,128)S(1)}, f32[128,256]{1,0:T(8,128)S(1)}, u32[]{:S(2)}, u32[]{:S(2)}) collective-permute-start(f32[128,256]{1,0:T(8,128)S(1)} %get-tuple-element.31), channel_id=1, source_target_pairs={{0,4},{4,8},{8,12},{1,5},{5,9},{9,13},{2,6},{6,10},{10,14},{3,7},{... | collective-permute-start | bytes 393224 | tf_op jit(solution)/shard_map/ppermute | solution.py:441
  19.5 0.0 copy-start.3
  19.5 0.7 %collective-permute-start.3 = (f32[128,256]{1,0:T(8,128)S(1)}, f32[128,256]{1,0:T(8,128)S(1)}, u32[]{:S(2)}, u32[]{:S(2)}) collective-permute-start(f32[128,256]{1,0:T(8,128)S(1)} %get-tuple-element.32), channel_id=1, source_target_pairs={{4,12},{5,13},{6,14},{7,15},{20,28},{21,29},{22,30},{23,31}} | collective-permute-start | bytes 393224 | tf_op jit(solution)/shard_map/ppermute | solution.py:442
  20.2 0.0 copy-done
  20.2 4.6 %local_part.3 = (bf16[2,2048,256]{2,1,0:T(8,128)(2,1)S(1)}, bf16[2,2048,256]{2,1,0:T(8,128)(2,1)S(1)}, f32[128,512]{1,0:T(8,128)}) custom-call(f32[8,4096]{1,0:T(8,128)S(1)} %copy-done.2, bf16[4096,128]{1,0:T(8,128)(2,1)S(1)} %copy-done.1, bf16[4096,512]{1,0:T(8,128)(2,1)S(1)} %copy-done, bf16[4096,128]{1,0:T(8,128)(2,1)S(1)} %get-tuple-element.25.entry_ref, ...), custom_call_target="tpu_custom_call" | custom-call | flops 1073741824 | bytes 9437184 | tf_op jit(solution)/shard_map/local_part/pallas_call | solution.py:244
  24.8 0.0 collective-permute-done.2.rest_1_.rest_0_
  24.8 0.0 copy-done.3
  24.8 2.6 %final_part.2.rest_8_ = bf16[4096,512]{1,0:T(8,128)(2,1)} custom-call(s32[1]{0:T(128)} %bitcast.place_ref, f32[128,256]{1,0:T(8,128)S(1)} %get-tuple-element.38.rest_0_, f32[128,256]{1,0:T(8,128)S(1)} %collective-permute-done.2.rest_1_.rest_0_, bf16[4096,128]{1,0:T(8,128)(2,1)S(1)} %copy-done.1, f32[2,1,256]{2,1,0:T(1,128)S(1)} %bitcast.2, ...), custom_call_target="tpu_custom_call" | custom-call | flops 536870912 | bytes 7340032 | tf_op jit(solution)/shard_map/final_part/pallas_call | solution.py:331
  27.5 0.0 collective-permute-done.3.rest_1_
  27.5 2.5 %final_part.3 = bf16[4096,512]{1,0:T(8,128)(2,1)} custom-call(s32[1]{0:T(128)} %bitcast.place_ref, f32[128,256]{1,0:T(8,128)S(1)} %collective-permute-done.2.rest_1_.rest_0_, f32[128,256]{1,0:T(8,128)S(1)} %collective-permute-done.3.rest_1_, bf16[4096,128]{1,0:T(8,128)(2,1)S(1)} %copy-done.1, ...), custom_call_target="tpu_custom_call", output_to_operand_aliasing={{}: (9, {})} | custom-call | flops 536870912 | bytes 7340032 | tf_op jit(solution)/shard_map/final_part/pallas_call | solution.py:331
  (1 shorter events, 0.0 us)
Async XLA Ops:
  0.0 11.3 %copy-start.1 = (bf16[4096,128]{1,0:T(8,128)(2,1)S(1)}, bf16[4096,128]{1,0:T(8,128)(2,1)}, u32[]{:S(2)}) copy-start(bf16[4096,128]{1,0:T(8,128)(2,1)} %rest_2_.3) | copy-start | bytes 3145732
  0.0 11.3 %copy-start.2 = (f32[8,4096]{1,0:T(8,128)S(1)}, f32[8,4096]{1,0:T(8,128)}, u32[]{:S(2)}) copy-start(f32[8,4096]{1,0:T(8,128)} %decay_ref.3) | copy-start | bytes 393220
  4.0 11.7 %collective-permute-start = (f32[136,256]{1,0:T(8,128)S(1)}, f32[136,256]{1,0:T(8,128)S(1)}, u32[]{:S(2)}, u32[]{:S(2)}) collective-permute-start(f32[136,256]{1,0:T(8,128)S(1)} %get-tuple-element.22), channel_id=1, source_target_pairs={{0,4},{4,8},{1,5},{5,9},{2,6},{6,10},{3,7},{7,11},{16,20},{20,24},... | collective-permute-start | bytes 417800 | tf_op jit(solution)/shard_map/ppermute | solution.py:435
  9.0 6.8 %collective-permute-start.1 = (f32[136,256]{1,0:T(8,128)S(1)}, f32[136,256]{1,0:T(8,128)S(1)}, u32[]{:S(2)}, u32[]{:S(2)}) collective-permute-start(f32[136,256]{1,0:T(8,128)S(1)} %get-tuple-element.23), channel_id=1, source_target_pairs={{8,4},{0,8},{9,5},{1,9},{10,6},{2,10},{11,7},{3,11},{24,20},{16,24... | collective-permute-start | bytes 417800 | tf_op jit(solution)/shard_map/ppermute | solution.py:436
  11.3 8.9 %copy-start = (bf16[4096,512]{1,0:T(8,128)(2,1)S(1)}, bf16[4096,512]{1,0:T(8,128)(2,1)}, u32[]{:S(2)}) copy-start(bf16[4096,512]{1,0:T(8,128)(2,1)} %gate_ref.1) | copy-start | bytes 12582916
  15.8 9.0 %collective-permute-start.2 = (f32[128,256]{1,0:T(8,128)S(1)}, f32[128,256]{1,0:T(8,128)S(1)}, u32[]{:S(2)}, u32[]{:S(2)}) collective-permute-start(f32[128,256]{1,0:T(8,128)S(1)} %get-tuple-element.31), channel_id=1, source_target_pairs={{0,4},{4,8},{8,12},{1,5},{5,9},{9,13},{2,6},{6,10},{10,14},{3,7},{... | collective-permute-start | bytes 393224 | tf_op jit(solution)/shard_map/ppermute | solution.py:441
  19.5 5.3 %copy-start.3 = (f32[512]{0:T(512)S(1)}, f32[512]{0:T(512)}, u32[]{:S(2)}) copy-start(f32[512]{0:T(512)} %param.11) | copy-start | bytes 6148
  19.5 7.9 %collective-permute-start.3 = (f32[128,256]{1,0:T(8,128)S(1)}, f32[128,256]{1,0:T(8,128)S(1)}, u32[]{:S(2)}, u32[]{:S(2)}) collective-permute-start(f32[128,256]{1,0:T(8,128)S(1)} %get-tuple-element.32), channel_id=1, source_target_pairs={{4,12},{5,13},{6,14},{7,15},{20,28},{21,29},{22,30},{23,31}} | collective-permute-start | bytes 393224 | tf_op jit(solution)/shard_map/ppermute | solution.py:442

commit v5 on v4

--- a/solution.py
+++ b/solution.py
@@ -127,7 +127,7 @@
     gate_copy.wait()
 
 
-def local_states(place, decay, entry_map, signal, gate_input, head_size, split, pieces, parts):
+def local_states(place, decay, entry_map, signal, gate_input, head_size, split, pieces, gate_rows):
     length, width = signal.shape
     state_size = entry_map.shape[1]
     tall = state_size + HEAD_ROWS
@@ -143,7 +143,7 @@
         + [
             pltpu.VMEM((length, state_size), BF16),
             pltpu.VMEM((length, width), BF16),
-            pltpu.VMEM((length // parts, width), BF16),
+            pltpu.VMEM((gate_rows, width), BF16),
         ],
         scratch_shapes=[
             pltpu.VMEM((HEAD_ROWS, length), F32),
@@ -168,7 +168,7 @@
 def local_kernel(base, head_size, group, decay_ref, readout_ref, gate_ref, entry_ref, signal_ref, state_in, *rest):
     inside_ref, share_ref, state_ref, in_ref, out_ref = rest
     length, width = signal_ref.shape
-    sides, part_rows, side = inside_ref.shape
+    part_rows = inside_ref.shape[0]
     first = base // CHUNK
     many = part_rows // CHUNK
     spread = spread_matrix(width, head_size)
@@ -188,8 +188,9 @@
         onward = part[:, 2 * CHUNK : 2 * CHUNK + HEAD_ROWS]
         if c >= first:
             from_middle = part[:, :CHUNK]
-            in_ref[c - first] = pair_rows(jnp.exp(-from_middle))
-            out_ref[c - first] = pair_rows(jnp.exp(from_middle))
+            frames = slice((c - first) * CHUNK, (c - first + 1) * CHUNK)
+            in_ref[:, frames] = pair_rows(jnp.exp(-from_middle))
+            out_ref[:, frames] = pair_rows(jnp.exp(from_middle))
             to_here.append(pair_rows(jnp.exp(before + to_middle)))
             if (c + 1) * CHUNK < length:
                 following = three[(c + 1) * HEAD_ROWS : (c + 2) * HEAD_ROWS, CHUNK : CHUNK + HEAD_ROWS]
@@ -200,19 +201,19 @@
     causal = s_from >= s_to
     state = state_in[...] if base else jnp.zeros(state_ref.shape, F32)
     for start in range(0, many, group):
-        here = range(start, start + group)
-        where = pl.ds(base + start * CHUNK, group * CHUNK)
-        there = pl.ds(start * CHUNK, group * CHUNK)
+        count = min(group, many - start)
+        where = pl.ds(base + start * CHUNK, count * CHUNK)
+        there = pl.ds(start * CHUNK, count * CHUNK)
         cut = lambda value, j: value[j * CHUNK : (j + 1) * CHUNK]
         entry = entry_ref[where, :]
         readout = readout_ref[where, :]
-        scaled = (signal_ref[where, :].astype(F32) * spread_rows(in_ref, here, spread)).astype(BF16)
+        scaled = (signal_ref[where, :].astype(F32) * mm(in_ref[:, there], spread, TN)).astype(BF16)
         scores, added, passed = [], [], []
-        for j in range(group):
+        for j in range(count):
             products = mm(cut(readout, j), cut(entry, j), NT)
             scores.append(jnp.where(causal, products, 0.0).astype(BF16))
             added.append(mm(cut(entry, j), cut(scaled, j), TN))
-        for j in range(group):
+        for j in range(count):
             passed.append(state.astype(BF16))
             state = by_head(state + added[j], mm(to_next[start + j], spread, TN))
         output = jnp.concatenate(
@@ -221,123 +222,116 @@
                     jnp.concatenate([scores[j], cut(readout, j)], axis=1),
                     jnp.concatenate([cut(scaled, j), passed[j]], axis=0),
                 )
-                for j in range(group)
+                for j in range(count)
             ],
             axis=0,
         )
         gate = gate_ref[there if gate_ref.shape[0] == part_rows else where, :].astype(F32)
-        opened = gate / (1.0 + jnp.exp(-gate)) * spread_rows(out_ref, here, spread)
-        inside = (output * opened).astype(BF16)
-        share = jnp.concatenate(
-            [by_head(cut(opened, j), mm(to_here[start + j], spread, TN)) for j in range(group)], axis=0
+        opened = gate / (1.0 + jnp.exp(-gate)) * mm(out_ref[:, there], spread, TN)
+        inside_ref[there, :] = (output * opened).astype(BF16)
+        share_ref[there, :] = jnp.concatenate(
+            [by_head(cut(opened, j), mm(to_here[start + j], spread, TN)) for j in range(count)], axis=0
         ).astype(BF16)
-        for k in range(sides):
-            inside_ref[k, there, :] = inside[:, k * side : (k + 1) * side]
-            share_ref[k, there, :] = share[:, k * side : (k + 1) * side]
     state_ref[...] = state
 
 
-def local_part(index, parts, decay, readout, gate_input, entry_map, signal, state, head_size, sides, group):
+def local_part(base, rows, decay, readout, gate_input, entry_map, signal, state, head_size, group):
     length, width = signal.shape
     state_size = entry_map.shape[1]
-    rows = length // parts
     return pl.pallas_call(
-        functools.partial(local_kernel, index * rows, head_size, group),
+        functools.partial(local_kernel, base, head_size, group),
         in_specs=[IN_VMEM] * 6,
         out_specs=[IN_VMEM] * 3,
-        out_shape=[pltpu.VMEM((sides, rows, width // sides), BF16)] * 2 + [pltpu.VMEM((state_size, width), F32)],
-        scratch_shapes=[pltpu.VMEM((rows // CHUNK, 2 * HEAD_ROWS, CHUNK), BF16)] * 2,
+        out_shape=[pltpu.VMEM((rows, width), BF16)] * 2 + [pltpu.VMEM((state_size, width), F32)],
+        scratch_shapes=[pltpu.VMEM((2 * HEAD_ROWS, rows), BF16)] * 2,
         name="local_part",
         compiler_params=pltpu.CompilerParams(vmem_limit_bytes=16 << 20),
         cost_estimate=pl.CostEstimate(
-            flops=8 * length * width * state_size // parts,
-            bytes_accessed=2 * length * (4 * width + 2 * state_size) // parts,
-            transcendentals=length * width // parts,
+            flops=8 * rows * width * state_size,
+            bytes_accessed=2 * rows * (4 * width + 2 * state_size),
+            transcendentals=rows * width,
         ),
     )(decay, readout, gate_input, entry_map, signal, state)
 
 
-def final_kernel(turn, head_size, parts, rows, place_ref, *rest):
-    count = 1 if turn is None else 2
+def final_kernel(count, head_size, parts, rows, place_ref, *rest):
     incoming, rest = rest[:count], rest[count:]
     readout_ref, gain_ref, *rest = rest
     groups, rest = [rest[2 * p : 2 * p + 2] for p in range(parts)], rest[2 * parts :]
-    result_hbm, result_ref, terms_ref, semaphores = rest[-4:]
+    result_hbm, result_ref, terms_ref, semaphores = rest
     size = readout_ref.shape[1]
-    _, part_rows, width = groups[0][0].shape
-
-    def keep(value):
-        high, low = two_terms(value)
-        terms_ref[:size, :] = high
-        terms_ref[size:, :] = low
-
-    if turn is None:
-        side = 0
-        keep(incoming[0][...])
+    width = gain_ref.shape[1]
+
+    def keep(value_ref, at):
+        high, low = two_terms(value_ref[...])
+        terms_ref[:size, at : at + value_ref.shape[1]] = high
+        terms_ref[size:, at : at + value_ref.shape[1]] = low
+
+    if count == 1:
+        keep(incoming[0], 0)
     else:
+        one, two, kept = incoming
         place = place_ref[0]
-        side = jnp.where(place == 1, turn, 1 - turn)
-        other = (place == 1) | (place == 2)
-
-        @pl.when(other)
-        def _():
-            keep(incoming[0][...])
-
-        @pl.when(jnp.logical_not(other))
-        def _():
-            keep(incoming[1][...])
+        half = width // 2
+
+        @pl.when(place == 1)
+        def _():
+            keep(kept, 0)
+            keep(one, half)
+
+        @pl.when(place == 2)
+        def _():
+            keep(one, 0)
+            keep(kept, half)
+
+        @pl.when((place != 1) & (place != 2))
+        def _():
+            keep(two, 0)
+            keep(one, half)
 
     group = min(width, 256)
     row = lax.broadcasted_iota(jnp.int32, (group, group), 0)
     column = lax.broadcasted_iota(jnp.int32, (group, group), 1)
     same = lax.div(row, head_size) == lax.div(column, head_size)
     average = jnp.where(same, 1.0 / head_size, 0.0).astype(BF16)
-    gain = gain_ref[side]
+    gain = gain_ref[...]
     terms = terms_ref[...]
-    columns = pl.ds(0, width) if turn is None else pl.ds(pl.multiple_of(side * width, width), width)
     copies = []
-    for p, (inside_ref, share_ref) in enumerate(groups):
-        for start in range(0, part_rows, rows):
-            where = pl.ds(start, rows)
-            there = pl.ds(p * part_rows + start, rows)
+    first = 0
+    for inside_ref, share_ref in groups:
+        for start in range(0, inside_ref.shape[0], rows):
+            many = min(rows, inside_ref.shape[0] - start)
+            where = pl.ds(start, many)
+            there = pl.ds(first + start, many)
             readout = readout_ref[there, :]
             across = mm(jnp.concatenate([readout, readout], axis=1), terms)
-            gated = inside_ref[side, where, :].astype(F32) + share_ref[side, where, :].astype(F32) * across
-            squares = (gated * gated).astype(BF16)
+            gated = inside_ref[where, :].astype(F32) + share_ref[where, :].astype(F32) * across
+            squares = gated.astype(BF16) * gated.astype(BF16)
             mean = jnp.concatenate(
                 [mm(squares[:, g : g + group], average) for g in range(0, width, group)], axis=1
             )
             result_ref[there, :] = (gated * lax.rsqrt(mean + EPSILON) * gain).astype(BF16)
-            copy = pltpu.make_async_copy(
-                result_ref.at[there], result_hbm.at[there, columns], semaphores.at[len(copies)]
-            )
+            copy = pltpu.make_async_copy(result_ref.at[there], result_hbm.at[there], semaphores.at[len(copies)])
             copy.start()
             copies.append(copy)
+        first += inside_ref.shape[0]
     for copy in copies:
         copy.wait()
 
 
-def final_part(turn, place, incoming, readout, norm_gain, groups, kept, head_size, rows):
-    sides, part_rows, width = groups[0][0].shape
-    length = part_rows * len(groups)
-    state_size = readout.shape[1]
+def final_part(place, incoming, readout, norm_gain, groups, head_size, rows):
+    length, state_size = readout.shape
+    width = norm_gain.shape[1]
     arguments = [place, *incoming, readout, norm_gain, *[v for g in groups for v in g]]
-    in_specs = [pl.BlockSpec(memory_space=pltpu.SMEM)] + [IN_VMEM] * (len(arguments) - 1)
-    aliases = {}
-    if kept is not None:
-        aliases = {len(arguments): 0}
-        arguments.append(kept)
-        in_specs.append(IN_HBM)
     return pl.pallas_call(
-        functools.partial(final_kernel, turn, head_size, len(groups), rows),
-        in_specs=in_specs,
+        functools.partial(final_kernel, len(incoming), head_size, len(groups), rows),
+        in_specs=[pl.BlockSpec(memory_space=pltpu.SMEM)] + [IN_VMEM] * (len(arguments) - 1),
         out_specs=IN_HBM,
-        out_shape=jax.ShapeDtypeStruct((length, width * sides), BF16),
-        input_output_aliases=aliases,
+        out_shape=jax.ShapeDtypeStruct((length, width), BF16),
         scratch_shapes=[
             pltpu.VMEM((length, width), BF16),
             pltpu.VMEM((2 * state_size, width), BF16),
-            pltpu.SemaphoreType.DMA((length // rows,)),
+            pltpu.SemaphoreType.DMA((length // rows + len(groups),)),
         ],
         name="final_part",
         compiler_params=pltpu.CompilerParams(vmem_limit_bytes=16 << 20),
@@ -420,13 +414,14 @@
     width = signal.shape[1]
     head_size = width // heads
     split = devices == 4 and width % 256 == 0
-    sides = 2 if split else 1
+    early = length * 10 // 16
+    late = length - early
     decay = log_decay
     if heads < HEAD_ROWS:
         decay = jnp.pad(log_decay, ((0, HEAD_ROWS - heads), (0, 0)))
     place = lax.axis_index("tm").astype(jnp.int32).reshape(1)
     *made, entry_map, signal, gate_first = local_states(
-        place, decay, entry_map, signal, gate_input, head_size, split, 4, 2
+        place, decay, entry_map, signal, gate_input, head_size, split, 4, early
     )
     common = (entry_map, signal)
     nothing = jnp.zeros((8, 128), F32)
@@ -434,20 +429,18 @@
         own, first, second = made
         one = lax.ppermute(first, "tm", [(0, 1), (1, 2)])
         two = lax.ppermute(second, "tm", [(2, 1), (0, 2)])
-    *before, state = local_part(0, 2, decay, readout, gate_first, *common, nothing, head_size, sides, 4)
+    *before, state = local_part(0, early, decay, readout, gate_first, *common, nothing, head_size, 8)
     if split:
         one, two, state = lax.optimization_barrier((one, two, state))
         first, second, kept = blend(place, one, two, own)
         one = lax.ppermute(first, "tm", [(0, 1), (1, 2), (2, 3)])
         two = lax.ppermute(second, "tm", [(1, 3)])
+        incoming = (one, two, kept)
     else:
-        total = scan_devices(made[0], devices)
-    *after, _ = local_part(1, 2, decay, readout, gate_input, *common, state, head_size, sides, 4)
-    common = (readout, norm_gain.reshape(sides, 1, width // sides), (before, after))
-    if split:
-        result = final_part(0, place, (kept, one), *common, None, head_size, 1024)
-        return final_part(1, place, (one, two), *common, result, head_size, 1024)
-    return final_part(None, place, (total,), *common, None, head_size, 1024)
+        incoming = (scan_devices(made[0], devices),)
+    *after, _ = local_part(early, late, decay, readout, gate_input, *common, state, head_size, 8)
+    gain = norm_gain.reshape(1, width)
+    return final_part(place, incoming, readout, gain, (before, after), head_size, 512)
 
 
 def solution(mesh):

time: 30.3 us -> 29.1 us (0.960)
  the two profiles are of different devices: /device:TPU:0 before, /device:TPU:30 now
where the time goes in v5:
time: 29.1 us; the launch traced here: 28.9 us
  Pallas kernels  17 us (58%)
  waiting for transfers between devices  7.61 us (26%)
  starting transfers between devices  3.92 us (13%)
    pallas_call x2, Pallas kernels, local_part(): pl.pallas_call(functools.partial(local_kernel, base, head_size, group), i...  8.83 us
    ppermute x1, waiting for transfers between devices, shards(): one = lax.ppermute(first, 'tm', [(0, 1), (1, 2), (2, 3)])  4.24 us
    pallas_call x1, Pallas kernels, final_part(): pl.pallas_call(functools.partial(final_kernel, len(incoming), head_size,...  4.14 us
    pallas_call x1, Pallas kernels, local_states(): pl.pallas_call(functools.partial(state_kernel, split, head_size, pieces),...  4.01 us
    ppermute x1, waiting for transfers between devices, shards(): two = lax.ppermute(second, 'tm', [(1, 3)])  3.37 us
    ppermute x1, starting transfers between devices, shards(): one = lax.ppermute(first, 'tm', [(0, 1), (1, 2), (2, 3)])  1.29 us
    ppermute x1, starting transfers between devices, shards(): two = lax.ppermute(second, 'tm', [(1, 3)])  1.29 us
    ppermute x1, starting transfers between devices, shards(): one = lax.ppermute(first, 'tm', [(0, 1), (1, 2)])  0.67 us
  transfers between devices with their start and end apart: 4, of which 2 were waited for; matrix products, arithmetic and copies ran while one was open for 0% of the time, Pallas kernels for 31%

profile of v5, /device:TPU:30, one launch (start us, length us, event | category | flops | bytes accessed | tf_op | source)
XLA Modules:
  0.0 28.9 jit_solution(13570875557362289736)
XLA Ops:
  0.0 0.0 copy-start.1
  0.0 0.0 copy-start.2
  0.0 4.0 %device_states.1 = (f32[2,136,256]{2,1,0:T(8,128)S(1)}, f32[136,256]{1,0:T(8,128)S(1)}, f32[136,256]{1,0:T(8,128)S(1)}, bf16[4096,128]{1,0:T(8,128)(2,1)S(1)}, b...) custom-call(s32[1]{0:T(128)} %bitcast.place_ref, f32[8,4096]{1,0:T(8,128)} %decay_ref.3, ...), custom_call_target="tpu_custom_call" | custom-call | flops 536870912 | bytes 5242880 | tf_op jit(solution)/shard_map/device_states/pallas_call | solution.py:138
  4.0 0.7 %collective-permute-start = (f32[136,256]{1,0:T(8,128)S(1)}, f32[136,256]{1,0:T(8,128)S(1)}, u32[]{:S(2)}, u32[]{:S(2)}) collective-permute-start(f32[136,256]{1,0:T(8,128)S(1)} %get-tuple-element.22), channel_id=1, source_target_pairs={{0,4},{4,8},{1,5},{5,9},{2,6},{6,10},{3,7},{7,11},{16,20},{20,24},... | collective-permute-start | bytes 417800 | tf_op jit(solution)/shard_map/ppermute | solution.py:430
  4.7 0.7 %collective-permute-start.1 = (f32[136,256]{1,0:T(8,128)S(1)}, f32[136,256]{1,0:T(8,128)S(1)}, u32[]{:S(2)}, u32[]{:S(2)}) collective-permute-start(f32[136,256]{1,0:T(8,128)S(1)} %get-tuple-element.23), channel_id=1, source_target_pairs={{8,4},{0,8},{9,5},{1,9},{10,6},{2,10},{11,7},{3,11},{24,20},{16,24... | collective-permute-start | bytes 417800 | tf_op jit(solution)/shard_map/ppermute | solution.py:431
  5.4 0.0 copy-done.1
  5.4 0.0 copy-done.2
  5.4 0.0 copy-start
  5.4 5.3 %local_part.2 = (bf16[2560,512]{1,0:T(8,128)(2,1)S(1)}, bf16[2560,512]{1,0:T(8,128)(2,1)S(1)}, f32[128,512]{1,0:T(8,128)S(1)}) custom-call(f32[8,4096]{1,0:T(8,128)S(1)} %copy-done.2, bf16[4096,128]{1,0:T(8,128)(2,1)S(1)} %copy-done.1, bf16[2560,512]{1,0:T(8,128)(2,1)S(1)} %get-tuple-element.24.gate_ref, bf16[4096,128]{1,0:T(8,128)(2,1)S(1)} %get-tuple-element.25.entry_ref, ...), custom_call_target="tpu_custom_call" | custom-call | flops 1342177280 | bytes 11796480 | tf_op jit(solution)/shard_map/local_part/pallas_call | solution.py:241
  10.7 0.0 collective-permute-done.one_ref
  10.7 0.0 collective-permute-done.1.two_ref
  10.7 0.1 blend.1
  10.8 1.3 %collective-permute-start.2 = (f32[128,256]{1,0:T(8,128)S(1)}, f32[128,256]{1,0:T(8,128)S(1)}, u32[]{:S(2)}, u32[]{:S(2)}) collective-permute-start(f32[128,256]{1,0:T(8,128)S(1)} %get-tuple-element.31), channel_id=1, source_target_pairs={{0,4},{4,8},{8,12},{1,5},{5,9},{9,13},{2,6},{6,10},{10,14},{3,7},{... | collective-permute-start | bytes 393224 | tf_op jit(solution)/shard_map/ppermute | solution.py:436
  12.1 0.0 copy-start.3
  12.1 1.3 %collective-permute-start.3 = (f32[128,256]{1,0:T(8,128)S(1)}, f32[128,256]{1,0:T(8,128)S(1)}, u32[]{:S(2)}, u32[]{:S(2)}) collective-permute-start(f32[128,256]{1,0:T(8,128)S(1)} %get-tuple-element.32), channel_id=1, source_target_pairs={{4,12},{5,13},{6,14},{7,15},{20,28},{21,29},{22,30},{23,31}} | collective-permute-start | bytes 393224 | tf_op jit(solution)/shard_map/ppermute | solution.py:437
  13.4 0.0 copy-done
  13.4 3.5 %local_part.3 = (bf16[1536,512]{1,0:T(8,128)(2,1)S(1)}, bf16[1536,512]{1,0:T(8,128)(2,1)S(1)}, f32[128,512]{1,0:T(8,128)}) custom-call(f32[8,4096]{1,0:T(8,128)S(1)} %copy-done.2, bf16[4096,128]{1,0:T(8,128)(2,1)S(1)} %copy-done.1, bf16[4096,512]{1,0:T(8,128)(2,1)S(1)} %copy-done, bf16[4096,128]{1,0:T(8,128)(2,1)S(1)} %get-tuple-element.25.entry_ref, ...), custom_call_target="tpu_custom_call" | custom-call | flops 805306368 | bytes 7077888 | tf_op jit(solution)/shard_map/local_part/pallas_call | solution.py:241
  17.0 4.2 %collective-permute-done.2.rest_0_ = f32[128,256]{1,0:T(8,128)S(1)} collective-permute-done((f32[128,256]{1,0:T(8,128)S(1)}, f32[128,256]{1,0:T(8,128)S(1)}, u32[]{:S(2)}, u32[]{:S(2)}) %collective-permute-start.2) | collective-permute-done | bytes 131104 | tf_op jit(solution)/shard_map/ppermute | solution.py:436
  21.2 3.4 %collective-permute-done.3.rest_1_ = f32[128,256]{1,0:T(8,128)S(1)} collective-permute-done((f32[128,256]{1,0:T(8,128)S(1)}, f32[128,256]{1,0:T(8,128)S(1)}, u32[]{:S(2)}, u32[]{:S(2)}) %collective-permute-start.3) | collective-permute-done | bytes 131104 | tf_op jit(solution)/shard_map/ppermute | solution.py:437
  24.6 0.0 copy-done.3
  24.6 4.1 %final_part.1 = bf16[4096,512]{1,0:T(8,128)(2,1)} custom-call(s32[1]{0:T(128)} %bitcast.place_ref, f32[128,256]{1,0:T(8,128)S(1)} %collective-permute-done.2.rest_0_, f32[128,256]{1,0:T(8,128)S(1)} %collective-permute-done.3.rest_1_, f32[128,256]{1,0:T(8,128)S(1)} %get-tuple-element.33.rest_2_, bf16[4096,128]{1,0:T(8,128)(2,1)S(1)} %copy-done.1, ...), custom_call_target="tpu_custom_call" | custom-call | flops 1073741824 | bytes 13631488 | tf_op jit(solution)/shard_map/final_part/pallas_call | solution.py:326
  (1 shorter events, 0.0 us)
Async XLA Ops:
  0.0 5.4 %copy-start.1 = (bf16[4096,128]{1,0:T(8,128)(2,1)S(1)}, bf16[4096,128]{1,0:T(8,128)(2,1)}, u32[]{:S(2)}) copy-start(bf16[4096,128]{1,0:T(8,128)(2,1)} %rest_3_.1) | copy-start | bytes 3145732
  0.0 5.4 %copy-start.2 = (f32[8,4096]{1,0:T(8,128)S(1)}, f32[8,4096]{1,0:T(8,128)}, u32[]{:S(2)}) copy-start(f32[8,4096]{1,0:T(8,128)} %decay_ref.3) | copy-start | bytes 393220
  4.0 6.7 %collective-permute-start = (f32[136,256]{1,0:T(8,128)S(1)}, f32[136,256]{1,0:T(8,128)S(1)}, u32[]{:S(2)}, u32[]{:S(2)}) collective-permute-start(f32[136,256]{1,0:T(8,128)S(1)} %get-tuple-element.22), channel_id=1, source_target_pairs={{0,4},{4,8},{1,5},{5,9},{2,6},{6,10},{3,7},{7,11},{16,20},{20,24},... | collective-permute-start | bytes 417800 | tf_op jit(solution)/shard_map/ppermute | solution.py:430
  4.7 6.0 %collective-permute-start.1 = (f32[136,256]{1,0:T(8,128)S(1)}, f32[136,256]{1,0:T(8,128)S(1)}, u32[]{:S(2)}, u32[]{:S(2)}) collective-permute-start(f32[136,256]{1,0:T(8,128)S(1)} %get-tuple-element.23), channel_id=1, source_target_pairs={{8,4},{0,8},{9,5},{1,9},{10,6},{2,10},{11,7},{3,11},{24,20},{16,24... | collective-permute-start | bytes 417800 | tf_op jit(solution)/shard_map/ppermute | solution.py:431
  5.4 8.0 %copy-start = (bf16[4096,512]{1,0:T(8,128)(2,1)S(1)}, bf16[4096,512]{1,0:T(8,128)(2,1)}, u32[]{:S(2)}) copy-start(bf16[4096,512]{1,0:T(8,128)(2,1)} %gate_ref.1) | copy-start | bytes 12582916
  10.8 10.4 %collective-permute-start.2 = (f32[128,256]{1,0:T(8,128)S(1)}, f32[128,256]{1,0:T(8,128)S(1)}, u32[]{:S(2)}, u32[]{:S(2)}) collective-permute-start(f32[128,256]{1,0:T(8,128)S(1)} %get-tuple-element.31), channel_id=1, source_target_pairs={{0,4},{4,8},{8,12},{1,5},{5,9},{9,13},{2,6},{6,10},{10,14},{3,7},{... | collective-permute-start | bytes 393224 | tf_op jit(solution)/shard_map/ppermute | solution.py:436
  12.1 12.5 %copy-start.3 = (f32[512]{0:T(512)S(1)}, f32[512]{0:T(512)}, u32[]{:S(2)}) copy-start(f32[512]{0:T(512)} %param.11) | copy-start | bytes 6148
  12.1 12.5 %collective-permute-start.3 = (f32[128,256]{1,0:T(8,128)S(1)}, f32[128,256]{1,0:T(8,128)S(1)}, u32[]{:S(2)}, u32[]{:S(2)}) collective-permute-start(f32[128,256]{1,0:T(8,128)S(1)} %get-tuple-element.32), channel_id=1, source_target_pairs={{4,12},{5,13},{6,14},{7,15},{20,28},{21,29},{22,30},{23,31}} | collective-permute-start | bytes 393224 | tf_op jit(solution)/shard_map/ppermute | solution.py:437

commit v6 on v5

--- a/solution.py
+++ b/solution.py
@@ -254,7 +254,7 @@
     )(decay, readout, gate_input, entry_map, signal, state)
 
 
-def final_kernel(count, head_size, parts, rows, place_ref, *rest):
+def final_kernel(count, head_size, parts, cuts, place_ref, *rest):
     incoming, rest = rest[:count], rest[count:]
     readout_ref, gain_ref, *rest = rest
     groups, rest = [rest[2 * p : 2 * p + 2] for p in range(parts)], rest[2 * parts :]
@@ -299,10 +299,10 @@
     copies = []
     first = 0
     for inside_ref, share_ref in groups:
+        rows = inside_ref.shape[0] // cuts
         for start in range(0, inside_ref.shape[0], rows):
-            many = min(rows, inside_ref.shape[0] - start)
-            where = pl.ds(start, many)
-            there = pl.ds(first + start, many)
+            where = pl.ds(start, rows)
+            there = pl.ds(first + start, rows)
             readout = readout_ref[there, :]
             across = mm(jnp.concatenate([readout, readout], axis=1), terms)
             gated = inside_ref[where, :].astype(F32) + share_ref[where, :].astype(F32) * across
@@ -319,19 +319,19 @@
         copy.wait()
 
 
-def final_part(place, incoming, readout, norm_gain, groups, head_size, rows):
+def final_part(place, incoming, readout, norm_gain, groups, head_size, cuts):
     length, state_size = readout.shape
     width = norm_gain.shape[1]
     arguments = [place, *incoming, readout, norm_gain, *[v for g in groups for v in g]]
     return pl.pallas_call(
-        functools.partial(final_kernel, len(incoming), head_size, len(groups), rows),
+        functools.partial(final_kernel, len(incoming), head_size, len(groups), cuts),
         in_specs=[pl.BlockSpec(memory_space=pltpu.SMEM)] + [IN_VMEM] * (len(arguments) - 1),
         out_specs=IN_HBM,
         out_shape=jax.ShapeDtypeStruct((length, width), BF16),
         scratch_shapes=[
             pltpu.VMEM((length, width), BF16),
             pltpu.VMEM((2 * state_size, width), BF16),
-            pltpu.SemaphoreType.DMA((length // rows + len(groups),)),
+            pltpu.SemaphoreType.DMA((len(groups) * cuts,)),
         ],
         name="final_part",
         compiler_params=pltpu.CompilerParams(vmem_limit_bytes=16 << 20),
@@ -414,7 +414,7 @@
     width = signal.shape[1]
     head_size = width // heads
     split = devices == 4 and width % 256 == 0
-    early = length * 10 // 16
+    early = length * 9 // 16
     late = length - early
     decay = log_decay
     if heads < HEAD_ROWS:
@@ -429,7 +429,7 @@
         own, first, second = made
         one = lax.ppermute(first, "tm", [(0, 1), (1, 2)])
         two = lax.ppermute(second, "tm", [(2, 1), (0, 2)])
-    *before, state = local_part(0, early, decay, readout, gate_first, *common, nothing, head_size, 8)
+    *before, state = local_part(0, early, decay, readout, gate_first, *common, nothing, head_size, early // (2 * CHUNK))
     if split:
         one, two, state = lax.optimization_barrier((one, two, state))
         first, second, kept = blend(place, one, two, own)
@@ -440,7 +440,7 @@
         incoming = (scan_devices(made[0], devices),)
     *after, _ = local_part(early, late, decay, readout, gate_input, *common, state, head_size, 8)
     gain = norm_gain.reshape(1, width)
-    return final_part(place, incoming, readout, gain, (before, after), head_size, 512)
+    return final_part(place, incoming, readout, gain, (before, after), head_size, 4)
 
 
 def solution(mesh):

time: 29.1 us -> 28.5 us (0.979)
  the two profiles are of different devices: /device:TPU:30 before, /device:TPU:0 now
where the time goes in v6:
time: 28.5 us; the launch traced here: 28.3 us
  Pallas kernels  16.5 us (58%)
  starting transfers between devices  11.4 us (40%)
  between operations  0.31 us (1%)
    pallas_call x2, Pallas kernels, local_part(): pl.pallas_call(functools.partial(local_kernel, base, head_size, group), i...  8.25 us
    ppermute x1, starting transfers between devices, shards(): one = lax.ppermute(first, 'tm', [(0, 1), (1, 2)])  4.93 us
    pallas_call x1, Pallas kernels, final_part(): pl.pallas_call(functools.partial(final_kernel, len(incoming), head_size,...  4.17 us
    pallas_call x1, Pallas kernels, local_states(): pl.pallas_call(functools.partial(state_kernel, split, head_size, pieces),...  4.01 us
    ppermute x1, starting transfers between devices, shards(): one = lax.ppermute(first, 'tm', [(0, 1), (1, 2), (2, 3)])  3.52 us
    ppermute x1, starting transfers between devices, shards(): two = lax.ppermute(second, 'tm', [(2, 1), (0, 2)])  2.31 us
    ppermute x1, starting transfers between devices, shards(): two = lax.ppermute(second, 'tm', [(1, 3)])  0.67 us
  transfers between devices with their start and end apart: 4, of which 0 were waited for; matrix products, arithmetic and copies ran while one was open for 0% of the time, Pallas kernels for 29%

profile of v6, /device:TPU:0, one launch (start us, length us, event | category | flops | bytes accessed | tf_op | source)
XLA Modules:
  0.0 28.3 jit_solution(11655635027979356091)
XLA Ops:
  0.0 0.0 copy-start.1
  0.0 0.0 copy-start.2
  0.0 4.0 %device_states.1 = (f32[2,136,256]{2,1,0:T(8,128)S(1)}, f32[136,256]{1,0:T(8,128)S(1)}, f32[136,256]{1,0:T(8,128)S(1)}, bf16[4096,128]{1,0:T(8,128)(2,1)S(1)}, b...) custom-call(s32[1]{0:T(128)} %bitcast.place_ref, f32[8,4096]{1,0:T(8,128)} %decay_ref.3, ...), custom_call_target="tpu_custom_call" | custom-call | flops 536870912 | bytes 5242880 | tf_op jit(solution)/shard_map/device_states/pallas_call | solution.py:138
  4.0 4.9 %collective-permute-start = (f32[136,256]{1,0:T(8,128)S(1)}, f32[136,256]{1,0:T(8,128)S(1)}, u32[]{:S(2)}, u32[]{:S(2)}) collective-permute-start(f32[136,256]{1,0:T(8,128)S(1)} %get-tuple-element.22), channel_id=1, source_target_pairs={{0,4},{4,8},{1,5},{5,9},{2,6},{6,10},{3,7},{7,11},{16,20},{20,24},... | collective-permute-start | bytes 417800 | tf_op jit(solution)/shard_map/ppermute | solution.py:430
  9.0 2.3 %collective-permute-start.1 = (f32[136,256]{1,0:T(8,128)S(1)}, f32[136,256]{1,0:T(8,128)S(1)}, u32[]{:S(2)}, u32[]{:S(2)}) collective-permute-start(f32[136,256]{1,0:T(8,128)S(1)} %get-tuple-element.23), channel_id=1, source_target_pairs={{8,4},{0,8},{9,5},{1,9},{10,6},{2,10},{11,7},{3,11},{24,20},{16,24... | collective-permute-start | bytes 417800 | tf_op jit(solution)/shard_map/ppermute | solution.py:431
  11.3 0.0 copy-done.1
  11.3 0.0 copy-done.2
  11.3 0.0 copy-start
  11.3 4.6 %local_part.2 = (bf16[2304,512]{1,0:T(8,128)(2,1)S(1)}, bf16[2304,512]{1,0:T(8,128)(2,1)S(1)}, f32[128,512]{1,0:T(8,128)S(1)}) custom-call(f32[8,4096]{1,0:T(8,128)S(1)} %copy-done.2, bf16[4096,128]{1,0:T(8,128)(2,1)S(1)} %copy-done.1, bf16[2304,512]{1,0:T(8,128)(2,1)S(1)} %get-tuple-element.24.gate_ref, bf16[4096,128]{1,0:T(8,128)(2,1)S(1)} %get-tuple-element.25.entry_ref, ...), custom_call_target="tpu_custom_call" | custom-call | flops 1207959552 | bytes 10616832 | tf_op jit(solution)/shard_map/local_part/pallas_call | solution.py:241
  15.9 0.0 collective-permute-done.one_ref
  15.9 0.0 collective-permute-done.1.two_ref
  15.9 0.1 blend.1
  16.0 3.5 %collective-permute-start.2 = (f32[128,256]{1,0:T(8,128)S(1)}, f32[128,256]{1,0:T(8,128)S(1)}, u32[]{:S(2)}, u32[]{:S(2)}) collective-permute-start(f32[128,256]{1,0:T(8,128)S(1)} %get-tuple-element.31), channel_id=1, source_target_pairs={{0,4},{4,8},{8,12},{1,5},{5,9},{9,13},{2,6},{6,10},{10,14},{3,7},{... | collective-permute-start | bytes 393224 | tf_op jit(solution)/shard_map/ppermute | solution.py:436
  19.5 0.0 copy-start.3
  19.5 0.7 %collective-permute-start.3 = (f32[128,256]{1,0:T(8,128)S(1)}, f32[128,256]{1,0:T(8,128)S(1)}, u32[]{:S(2)}, u32[]{:S(2)}) collective-permute-start(f32[128,256]{1,0:T(8,128)S(1)} %get-tuple-element.32), channel_id=1, source_target_pairs={{4,12},{5,13},{6,14},{7,15},{20,28},{21,29},{22,30},{23,31}} | collective-permute-start | bytes 393224 | tf_op jit(solution)/shard_map/ppermute | solution.py:437
  20.2 0.0 copy-done
  20.2 3.7 %local_part.3 = (bf16[1792,512]{1,0:T(8,128)(2,1)S(1)}, bf16[1792,512]{1,0:T(8,128)(2,1)S(1)}, f32[128,512]{1,0:T(8,128)}) custom-call(f32[8,4096]{1,0:T(8,128)S(1)} %copy-done.2, bf16[4096,128]{1,0:T(8,128)(2,1)S(1)} %copy-done.1, bf16[4096,512]{1,0:T(8,128)(2,1)S(1)} %copy-done, bf16[4096,128]{1,0:T(8,128)(2,1)S(1)} %get-tuple-element.25.entry_ref, ...), custom_call_target="tpu_custom_call" | custom-call | flops 939524096 | bytes 8257536 | tf_op jit(solution)/shard_map/local_part/pallas_call | solution.py:241
  23.9 0.0 collective-permute-done.2.rest_0_
  23.9 0.0 collective-permute-done.3.rest_1_
  23.9 0.0 copy-done.3
  23.9 4.2 %final_part.1 = bf16[4096,512]{1,0:T(8,128)(2,1)} custom-call(s32[1]{0:T(128)} %bitcast.place_ref, f32[128,256]{1,0:T(8,128)S(1)} %collective-permute-done.2.rest_0_, f32[128,256]{1,0:T(8,128)S(1)} %collective-permute-done.3.rest_1_, f32[128,256]{1,0:T(8,128)S(1)} %get-tuple-element.33.rest_2_, bf16[4096,128]{1,0:T(8,128)(2,1)S(1)} %copy-done.1, ...), custom_call_target="tpu_custom_call" | custom-call | flops 1073741824 | bytes 13631488 | tf_op jit(solution)/shard_map/final_part/pallas_call | solution.py:326
  (1 shorter events, 0.0 us)
Async XLA Ops:
  0.0 11.3 %copy-start.1 = (bf16[4096,128]{1,0:T(8,128)(2,1)S(1)}, bf16[4096,128]{1,0:T(8,128)(2,1)}, u32[]{:S(2)}) copy-start(bf16[4096,128]{1,0:T(8,128)(2,1)} %rest_3_.1) | copy-start | bytes 3145732
  0.0 11.3 %copy-start.2 = (f32[8,4096]{1,0:T(8,128)S(1)}, f32[8,4096]{1,0:T(8,128)}, u32[]{:S(2)}) copy-start(f32[8,4096]{1,0:T(8,128)} %decay_ref.3) | copy-start | bytes 393220
  4.0 11.9 %collective-permute-start = (f32[136,256]{1,0:T(8,128)S(1)}, f32[136,256]{1,0:T(8,128)S(1)}, u32[]{:S(2)}, u32[]{:S(2)}) collective-permute-start(f32[136,256]{1,0:T(8,128)S(1)} %get-tuple-element.22), channel_id=1, source_target_pairs={{0,4},{4,8},{1,5},{5,9},{2,6},{6,10},{3,7},{7,11},{16,20},{20,24},... | collective-permute-start | bytes 417800 | tf_op jit(solution)/shard_map/ppermute | solution.py:430
  9.0 7.0 %collective-permute-start.1 = (f32[136,256]{1,0:T(8,128)S(1)}, f32[136,256]{1,0:T(8,128)S(1)}, u32[]{:S(2)}, u32[]{:S(2)}) collective-permute-start(f32[136,256]{1,0:T(8,128)S(1)} %get-tuple-element.23), channel_id=1, source_target_pairs={{8,4},{0,8},{9,5},{1,9},{10,6},{2,10},{11,7},{3,11},{24,20},{16,24... | collective-permute-start | bytes 417800 | tf_op jit(solution)/shard_map/ppermute | solution.py:431
  11.3 8.9 %copy-start = (bf16[4096,512]{1,0:T(8,128)(2,1)S(1)}, bf16[4096,512]{1,0:T(8,128)(2,1)}, u32[]{:S(2)}) copy-start(bf16[4096,512]{1,0:T(8,128)(2,1)} %gate_ref.1) | copy-start | bytes 12582916
  16.0 7.9 %collective-permute-start.2 = (f32[128,256]{1,0:T(8,128)S(1)}, f32[128,256]{1,0:T(8,128)S(1)}, u32[]{:S(2)}, u32[]{:S(2)}) collective-permute-start(f32[128,256]{1,0:T(8,128)S(1)} %get-tuple-element.31), channel_id=1, source_target_pairs={{0,4},{4,8},{8,12},{1,5},{5,9},{9,13},{2,6},{6,10},{10,14},{3,7},{... | collective-permute-start | bytes 393224 | tf_op jit(solution)/shard_map/ppermute | solution.py:436
  19.5 4.4 %copy-start.3 = (f32[512]{0:T(512)S(1)}, f32[512]{0:T(512)}, u32[]{:S(2)}) copy-start(f32[512]{0:T(512)} %param.11) | copy-start | bytes 6148
  19.5 4.4 %collective-permute-start.3 = (f32[128,256]{1,0:T(8,128)S(1)}, f32[128,256]{1,0:T(8,128)S(1)}, u32[]{:S(2)}, u32[]{:S(2)}) collective-permute-start(f32[128,256]{1,0:T(8,128)S(1)} %get-tuple-element.32), channel_id=1, source_target_pairs={{4,12},{5,13},{6,14},{7,15},{20,28},{21,29},{22,30},{23,31}} | collective-permute-start | bytes 393224 | tf_op jit(solution)/shard_map/ppermute | solution.py:437

commit v7 on v6

--- a/solution.py
+++ b/solution.py
@@ -172,28 +172,29 @@
     first = base // CHUNK
     many = part_rows // CHUNK
     spread = spread_matrix(width, head_size)
-    tall = stacked(decay_ref[...])
+    needed = min(first + many + 1, length // CHUNK)
+    tall = stacked(decay_ref[:, : needed * CHUNK])
     half = CHUNK // 2
     s_from = lax.broadcasted_iota(jnp.int32, (CHUNK, CHUNK), 0)
     s_to = lax.broadcasted_iota(jnp.int32, (CHUNK, CHUNK), 1)
     early = (s_from < half).astype(F32)
     centred = ((s_from <= s_to).astype(F32) - early).astype(BF16)
-    matrix = jnp.concatenate([centred, early.astype(BF16), (1.0 - early).astype(BF16)], axis=1)
-    three = sums(tall, matrix)
+    halves = sums(tall, jnp.concatenate([early.astype(BF16), (1.0 - early).astype(BF16)], axis=1))
+    inner = sums(tall[first * HEAD_ROWS : (first + many) * HEAD_ROWS], centred)
     before = jnp.zeros((HEAD_ROWS, HEAD_ROWS), F32)
     to_here, to_next = [], []
     for c in range(first + many):
-        part = three[c * HEAD_ROWS : (c + 1) * HEAD_ROWS]
-        to_middle = part[:, CHUNK : CHUNK + HEAD_ROWS]
-        onward = part[:, 2 * CHUNK : 2 * CHUNK + HEAD_ROWS]
+        part = halves[c * HEAD_ROWS : (c + 1) * HEAD_ROWS]
+        to_middle = part[:, :HEAD_ROWS]
+        onward = part[:, CHUNK : CHUNK + HEAD_ROWS]
         if c >= first:
-            from_middle = part[:, :CHUNK]
+            from_middle = inner[(c - first) * HEAD_ROWS : (c - first + 1) * HEAD_ROWS]
             frames = slice((c - first) * CHUNK, (c - first + 1) * CHUNK)
             in_ref[:, frames] = pair_rows(jnp.exp(-from_middle))
             out_ref[:, frames] = pair_rows(jnp.exp(from_middle))
             to_here.append(pair_rows(jnp.exp(before + to_middle)))
             if (c + 1) * CHUNK < length:
-                following = three[(c + 1) * HEAD_ROWS : (c + 2) * HEAD_ROWS, CHUNK : CHUNK + HEAD_ROWS]
+                following = halves[(c + 1) * HEAD_ROWS : (c + 2) * HEAD_ROWS, :HEAD_ROWS]
                 to_next.append(pair_rows(jnp.exp(onward + following)))
             else:
                 to_next.append(pair_rows(jnp.exp(onward)))

time: 28.5 us -> 28.5 us (level)
  no operation moved by 1% of the time
where the time goes in v7:
time: 28.5 us; the launch traced here: 28.3 us
  Pallas kernels  16.6 us (58%)
  starting transfers between devices  11.4 us (40%)
  between operations  0.31 us (1%)
    pallas_call x2, Pallas kernels, local_part(): pl.pallas_call(functools.partial(local_kernel, base, head_size, group), i...  8.34 us
    ppermute x1, starting transfers between devices, shards(): one = lax.ppermute(first, 'tm', [(0, 1), (1, 2)])  4.93 us
    pallas_call x1, Pallas kernels, final_part(): pl.pallas_call(functools.partial(final_kernel, len(incoming), head_size,...  4.16 us
    pallas_call x1, Pallas kernels, local_states(): pl.pallas_call(functools.partial(state_kernel, split, head_size, pieces),...  4.01 us
    ppermute x1, starting transfers between devices, shards(): one = lax.ppermute(first, 'tm', [(0, 1), (1, 2), (2, 3)])  3.51 us
    ppermute x1, starting transfers between devices, shards(): two = lax.ppermute(second, 'tm', [(2, 1), (0, 2)])  2.31 us
    ppermute x1, starting transfers between devices, shards(): two = lax.ppermute(second, 'tm', [(1, 3)])  0.67 us
  transfers between devices with their start and end apart: 4, of which 0 were waited for; matrix products, arithmetic and copies ran while one was open for 0% of the time, Pallas kernels for 29%

profile of v7, /device:TPU:0, one launch (start us, length us, event | category | flops | bytes accessed | tf_op | source)
XLA Modules:
  0.0 28.3 jit_solution(1301922678059119191)
XLA Ops:
  0.0 0.0 copy-start.1
  0.0 0.0 copy-start.2
  0.0 4.0 %device_states.1 = (f32[2,136,256]{2,1,0:T(8,128)S(1)}, f32[136,256]{1,0:T(8,128)S(1)}, f32[136,256]{1,0:T(8,128)S(1)}, bf16[4096,128]{1,0:T(8,128)(2,1)S(1)}, b...) custom-call(s32[1]{0:T(128)} %bitcast.place_ref, f32[8,4096]{1,0:T(8,128)} %decay_ref.3, ...), custom_call_target="tpu_custom_call" | custom-call | flops 536870912 | bytes 5242880 | tf_op jit(solution)/shard_map/device_states/pallas_call | solution.py:138
  4.0 4.9 %collective-permute-start = (f32[136,256]{1,0:T(8,128)S(1)}, f32[136,256]{1,0:T(8,128)S(1)}, u32[]{:S(2)}, u32[]{:S(2)}) collective-permute-start(f32[136,256]{1,0:T(8,128)S(1)} %get-tuple-element.22), channel_id=1, source_target_pairs={{0,4},{4,8},{1,5},{5,9},{2,6},{6,10},{3,7},{7,11},{16,20},{20,24},... | collective-permute-start | bytes 417800 | tf_op jit(solution)/shard_map/ppermute | solution.py:431
  9.0 2.3 %collective-permute-start.1 = (f32[136,256]{1,0:T(8,128)S(1)}, f32[136,256]{1,0:T(8,128)S(1)}, u32[]{:S(2)}, u32[]{:S(2)}) collective-permute-start(f32[136,256]{1,0:T(8,128)S(1)} %get-tuple-element.23), channel_id=1, source_target_pairs={{8,4},{0,8},{9,5},{1,9},{10,6},{2,10},{11,7},{3,11},{24,20},{16,24... | collective-permute-start | bytes 417800 | tf_op jit(solution)/shard_map/ppermute | solution.py:432
  11.3 0.0 copy-done.1
  11.3 0.0 copy-done.2
  11.3 0.0 copy-start
  11.3 4.6 %local_part.2 = (bf16[2304,512]{1,0:T(8,128)(2,1)S(1)}, bf16[2304,512]{1,0:T(8,128)(2,1)S(1)}, f32[128,512]{1,0:T(8,128)S(1)}) custom-call(f32[8,4096]{1,0:T(8,128)S(1)} %copy-done.2, bf16[4096,128]{1,0:T(8,128)(2,1)S(1)} %copy-done.1, bf16[2304,512]{1,0:T(8,128)(2,1)S(1)} %get-tuple-element.24.gate_ref, bf16[4096,128]{1,0:T(8,128)(2,1)S(1)} %get-tuple-element.25.entry_ref, ...), custom_call_target="tpu_custom_call" | custom-call | flops 1207959552 | bytes 10616832 | tf_op jit(solution)/shard_map/local_part/pallas_call | solution.py:242
  15.9 0.0 collective-permute-done.one_ref
  15.9 0.0 collective-permute-done.1.two_ref
  15.9 0.1 blend.1
  16.0 3.5 %collective-permute-start.2 = (f32[128,256]{1,0:T(8,128)S(1)}, f32[128,256]{1,0:T(8,128)S(1)}, u32[]{:S(2)}, u32[]{:S(2)}) collective-permute-start(f32[128,256]{1,0:T(8,128)S(1)} %get-tuple-element.31), channel_id=1, source_target_pairs={{0,4},{4,8},{8,12},{1,5},{5,9},{9,13},{2,6},{6,10},{10,14},{3,7},{... | collective-permute-start | bytes 393224 | tf_op jit(solution)/shard_map/ppermute | solution.py:437
  19.5 0.0 copy-start.3
  19.5 0.7 %collective-permute-start.3 = (f32[128,256]{1,0:T(8,128)S(1)}, f32[128,256]{1,0:T(8,128)S(1)}, u32[]{:S(2)}, u32[]{:S(2)}) collective-permute-start(f32[128,256]{1,0:T(8,128)S(1)} %get-tuple-element.32), channel_id=1, source_target_pairs={{4,12},{5,13},{6,14},{7,15},{20,28},{21,29},{22,30},{23,31}} | collective-permute-start | bytes 393224 | tf_op jit(solution)/shard_map/ppermute | solution.py:438
  20.2 0.0 copy-done
  20.2 3.7 %local_part.3 = (bf16[1792,512]{1,0:T(8,128)(2,1)S(1)}, bf16[1792,512]{1,0:T(8,128)(2,1)S(1)}, f32[128,512]{1,0:T(8,128)}) custom-call(f32[8,4096]{1,0:T(8,128)S(1)} %copy-done.2, bf16[4096,128]{1,0:T(8,128)(2,1)S(1)} %copy-done.1, bf16[4096,512]{1,0:T(8,128)(2,1)S(1)} %copy-done, bf16[4096,128]{1,0:T(8,128)(2,1)S(1)} %get-tuple-element.25.entry_ref, ...), custom_call_target="tpu_custom_call" | custom-call | flops 939524096 | bytes 8257536 | tf_op jit(solution)/shard_map/local_part/pallas_call | solution.py:242
  24.0 0.0 collective-permute-done.2.rest_0_
  24.0 0.0 collective-permute-done.3.rest_1_
  24.0 0.0 copy-done.3
  24.0 4.2 %final_part.1 = bf16[4096,512]{1,0:T(8,128)(2,1)} custom-call(s32[1]{0:T(128)} %bitcast.place_ref, f32[128,256]{1,0:T(8,128)S(1)} %collective-permute-done.2.rest_0_, f32[128,256]{1,0:T(8,128)S(1)} %collective-permute-done.3.rest_1_, f32[128,256]{1,0:T(8,128)S(1)} %get-tuple-element.33.rest_2_, bf16[4096,128]{1,0:T(8,128)(2,1)S(1)} %copy-done.1, ...), custom_call_target="tpu_custom_call" | custom-call | flops 1073741824 | bytes 13631488 | tf_op jit(solution)/shard_map/final_part/pallas_call | solution.py:327
  (1 shorter events, 0.0 us)
Async XLA Ops:
  0.0 11.3 %copy-start.1 = (bf16[4096,128]{1,0:T(8,128)(2,1)S(1)}, bf16[4096,128]{1,0:T(8,128)(2,1)}, u32[]{:S(2)}) copy-start(bf16[4096,128]{1,0:T(8,128)(2,1)} %rest_3_.1) | copy-start | bytes 3145732
  0.0 11.3 %copy-start.2 = (f32[8,4096]{1,0:T(8,128)S(1)}, f32[8,4096]{1,0:T(8,128)}, u32[]{:S(2)}) copy-start(f32[8,4096]{1,0:T(8,128)} %decay_ref.3) | copy-start | bytes 393220
  4.0 11.9 %collective-permute-start = (f32[136,256]{1,0:T(8,128)S(1)}, f32[136,256]{1,0:T(8,128)S(1)}, u32[]{:S(2)}, u32[]{:S(2)}) collective-permute-start(f32[136,256]{1,0:T(8,128)S(1)} %get-tuple-element.22), channel_id=1, source_target_pairs={{0,4},{4,8},{1,5},{5,9},{2,6},{6,10},{3,7},{7,11},{16,20},{20,24},... | collective-permute-start | bytes 417800 | tf_op jit(solution)/shard_map/ppermute | solution.py:431
  9.0 7.0 %collective-permute-start.1 = (f32[136,256]{1,0:T(8,128)S(1)}, f32[136,256]{1,0:T(8,128)S(1)}, u32[]{:S(2)}, u32[]{:S(2)}) collective-permute-start(f32[136,256]{1,0:T(8,128)S(1)} %get-tuple-element.23), channel_id=1, source_target_pairs={{8,4},{0,8},{9,5},{1,9},{10,6},{2,10},{11,7},{3,11},{24,20},{16,24... | collective-permute-start | bytes 417800 | tf_op jit(solution)/shard_map/ppermute | solution.py:432
  11.3 8.9 %copy-start = (bf16[4096,512]{1,0:T(8,128)(2,1)S(1)}, bf16[4096,512]{1,0:T(8,128)(2,1)}, u32[]{:S(2)}) copy-start(bf16[4096,512]{1,0:T(8,128)(2,1)} %gate_ref.1) | copy-start | bytes 12582916
  16.0 8.0 %collective-permute-start.2 = (f32[128,256]{1,0:T(8,128)S(1)}, f32[128,256]{1,0:T(8,128)S(1)}, u32[]{:S(2)}, u32[]{:S(2)}) collective-permute-start(f32[128,256]{1,0:T(8,128)S(1)} %get-tuple-element.31), channel_id=1, source_target_pairs={{0,4},{4,8},{8,12},{1,5},{5,9},{9,13},{2,6},{6,10},{10,14},{3,7},{... | collective-permute-start | bytes 393224 | tf_op jit(solution)/shard_map/ppermute | solution.py:437
  19.5 4.5 %copy-start.3 = (f32[512]{0:T(512)S(1)}, f32[512]{0:T(512)}, u32[]{:S(2)}) copy-start(f32[512]{0:T(512)} %param.11) | copy-start | bytes 6148
  19.5 4.4 %collective-permute-start.3 = (f32[128,256]{1,0:T(8,128)S(1)}, f32[128,256]{1,0:T(8,128)S(1)}, u32[]{:S(2)}, u32[]{:S(2)}) collective-permute-start(f32[128,256]{1,0:T(8,128)S(1)} %get-tuple-element.32), channel_id=1, source_target_pairs={{4,12},{5,13},{6,14},{7,15},{20,28},{21,29},{22,30},{23,31}} | collective-permute-start | bytes 393224 | tf_op jit(solution)/shard_map/ppermute | solution.py:438

commit v8 on v7

--- a/solution.py
+++ b/solution.py
@@ -111,15 +111,19 @@
             own_ref[k, :size, :] = states[:, k * half : (k + 1) * half]
             own_ref[k, size:, :] = gain[:, k * half : (k + 1) * half]
 
+        def fill(ref, k):
+            ref[:size, :] = states[:, k * half : (k + 1) * half]
+            ref[size:, :] = gain[:, k * half : (k + 1) * half]
+
         @pl.when(place_ref[0] == 0)
         def _():
-            first_ref[...] = own_ref[0]
-            second_ref[...] = own_ref[1]
+            fill(first_ref, 0)
+            fill(second_ref, 1)
 
         @pl.when(place_ref[0] != 0)
         def _():
-            first_ref[...] = own_ref[1]
-            second_ref[...] = own_ref[0]
+            fill(first_ref, 1)
+            fill(second_ref, 0)
     else:
         (own_ref,) = outs
         own_ref[:size, :] = states

time: 28.5 us -> 28.5 us (level)
  no operation moved by 1% of the time
where the time goes in v8:
time: 28.5 us; the launch traced here: 28.3 us
  Pallas kernels  16.6 us (58%)
  starting transfers between devices  11.4 us (40%)
  between operations  0.31 us (1%)
    pallas_call x2, Pallas kernels, local_part(): pl.pallas_call(functools.partial(local_kernel, base, head_size, group), i...  8.34 us
    ppermute x1, starting transfers between devices, shards(): one = lax.ppermute(first, 'tm', [(0, 1), (1, 2)])  4.94 us
    pallas_call x1, Pallas kernels, final_part(): pl.pallas_call(functools.partial(final_kernel, len(incoming), head_size,...  4.16 us
    pallas_call x1, Pallas kernels, local_states(): pl.pallas_call(functools.partial(state_kernel, split, head_size, pieces),...  4 us
    ppermute x1, starting transfers between devices, shards(): one = lax.ppermute(first, 'tm', [(0, 1), (1, 2), (2, 3)])  3.51 us
    ppermute x1, starting transfers between devices, shards(): two = lax.ppermute(second, 'tm', [(2, 1), (0, 2)])  2.31 us
    ppermute x1, starting transfers between devices, shards(): two = lax.ppermute(second, 'tm', [(1, 3)])  0.67 us
  transfers between devices with their start and end apart: 4, of which 0 were waited for; matrix products, arithmetic and copies ran while one was open for 0% of the time, Pallas kernels for 29%

profile of v8, /device:TPU:0, one launch (start us, length us, event | category | flops | bytes accessed | tf_op | source)
XLA Modules:
  0.0 28.3 jit_solution(8681371608515549734)
XLA Ops:
  0.0 0.0 copy-start.1
  0.0 0.0 copy-start.2
  0.0 4.0 %device_states.1 = (f32[2,136,256]{2,1,0:T(8,128)S(1)}, f32[136,256]{1,0:T(8,128)S(1)}, f32[136,256]{1,0:T(8,128)S(1)}, bf16[4096,128]{1,0:T(8,128)(2,1)S(1)}, b...) custom-call(s32[1]{0:T(128)} %bitcast.place_ref, f32[8,4096]{1,0:T(8,128)} %decay_ref.3, ...), custom_call_target="tpu_custom_call" | custom-call | flops 536870912 | bytes 5242880 | tf_op jit(solution)/shard_map/device_states/pallas_call | solution.py:142
  4.0 4.9 %collective-permute-start = (f32[136,256]{1,0:T(8,128)S(1)}, f32[136,256]{1,0:T(8,128)S(1)}, u32[]{:S(2)}, u32[]{:S(2)}) collective-permute-start(f32[136,256]{1,0:T(8,128)S(1)} %get-tuple-element.22), channel_id=1, source_target_pairs={{0,4},{4,8},{1,5},{5,9},{2,6},{6,10},{3,7},{7,11},{16,20},{20,24},... | collective-permute-start | bytes 417800 | tf_op jit(solution)/shard_map/ppermute | solution.py:435
  9.0 2.3 %collective-permute-start.1 = (f32[136,256]{1,0:T(8,128)S(1)}, f32[136,256]{1,0:T(8,128)S(1)}, u32[]{:S(2)}, u32[]{:S(2)}) collective-permute-start(f32[136,256]{1,0:T(8,128)S(1)} %get-tuple-element.23), channel_id=1, source_target_pairs={{8,4},{0,8},{9,5},{1,9},{10,6},{2,10},{11,7},{3,11},{24,20},{16,24... | collective-permute-start | bytes 417800 | tf_op jit(solution)/shard_map/ppermute | solution.py:436
  11.3 0.0 copy-done.1
  11.3 0.0 copy-done.2
  11.3 0.0 copy-start
  11.3 4.6 %local_part.2 = (bf16[2304,512]{1,0:T(8,128)(2,1)S(1)}, bf16[2304,512]{1,0:T(8,128)(2,1)S(1)}, f32[128,512]{1,0:T(8,128)S(1)}) custom-call(f32[8,4096]{1,0:T(8,128)S(1)} %copy-done.2, bf16[4096,128]{1,0:T(8,128)(2,1)S(1)} %copy-done.1, bf16[2304,512]{1,0:T(8,128)(2,1)S(1)} %get-tuple-element.24.gate_ref, bf16[4096,128]{1,0:T(8,128)(2,1)S(1)} %get-tuple-element.25.entry_ref, ...), custom_call_target="tpu_custom_call" | custom-call | flops 1207959552 | bytes 10616832 | tf_op jit(solution)/shard_map/local_part/pallas_call | solution.py:246
  15.9 0.0 collective-permute-done.one_ref
  15.9 0.0 collective-permute-done.1.two_ref
  15.9 0.1 blend.1
  16.0 3.5 %collective-permute-start.2 = (f32[128,256]{1,0:T(8,128)S(1)}, f32[128,256]{1,0:T(8,128)S(1)}, u32[]{:S(2)}, u32[]{:S(2)}) collective-permute-start(f32[128,256]{1,0:T(8,128)S(1)} %get-tuple-element.31), channel_id=1, source_target_pairs={{0,4},{4,8},{8,12},{1,5},{5,9},{9,13},{2,6},{6,10},{10,14},{3,7},{... | collective-permute-start | bytes 393224 | tf_op jit(solution)/shard_map/ppermute | solution.py:441
  19.5 0.0 copy-start.3
  19.5 0.7 %collective-permute-start.3 = (f32[128,256]{1,0:T(8,128)S(1)}, f32[128,256]{1,0:T(8,128)S(1)}, u32[]{:S(2)}, u32[]{:S(2)}) collective-permute-start(f32[128,256]{1,0:T(8,128)S(1)} %get-tuple-element.32), channel_id=1, source_target_pairs={{4,12},{5,13},{6,14},{7,15},{20,28},{21,29},{22,30},{23,31}} | collective-permute-start | bytes 393224 | tf_op jit(solution)/shard_map/ppermute | solution.py:442
  20.2 0.0 copy-done
  20.2 3.7 %local_part.3 = (bf16[1792,512]{1,0:T(8,128)(2,1)S(1)}, bf16[1792,512]{1,0:T(8,128)(2,1)S(1)}, f32[128,512]{1,0:T(8,128)}) custom-call(f32[8,4096]{1,0:T(8,128)S(1)} %copy-done.2, bf16[4096,128]{1,0:T(8,128)(2,1)S(1)} %copy-done.1, bf16[4096,512]{1,0:T(8,128)(2,1)S(1)} %copy-done, bf16[4096,128]{1,0:T(8,128)(2,1)S(1)} %get-tuple-element.25.entry_ref, ...), custom_call_target="tpu_custom_call" | custom-call | flops 939524096 | bytes 8257536 | tf_op jit(solution)/shard_map/local_part/pallas_call | solution.py:246
  24.0 0.0 collective-permute-done.2.rest_0_
  24.0 0.0 collective-permute-done.3.rest_1_
  24.0 0.0 copy-done.3
  24.0 4.2 %final_part.1 = bf16[4096,512]{1,0:T(8,128)(2,1)} custom-call(s32[1]{0:T(128)} %bitcast.place_ref, f32[128,256]{1,0:T(8,128)S(1)} %collective-permute-done.2.rest_0_, f32[128,256]{1,0:T(8,128)S(1)} %collective-permute-done.3.rest_1_, f32[128,256]{1,0:T(8,128)S(1)} %get-tuple-element.33.rest_2_, bf16[4096,128]{1,0:T(8,128)(2,1)S(1)} %copy-done.1, ...), custom_call_target="tpu_custom_call" | custom-call | flops 1073741824 | bytes 13631488 | tf_op jit(solution)/shard_map/final_part/pallas_call | solution.py:331
  (1 shorter events, 0.0 us)
Async XLA Ops:
  0.0 11.3 %copy-start.1 = (bf16[4096,128]{1,0:T(8,128)(2,1)S(1)}, bf16[4096,128]{1,0:T(8,128)(2,1)}, u32[]{:S(2)}) copy-start(bf16[4096,128]{1,0:T(8,128)(2,1)} %rest_3_.1) | copy-start | bytes 3145732
  0.0 11.3 %copy-start.2 = (f32[8,4096]{1,0:T(8,128)S(1)}, f32[8,4096]{1,0:T(8,128)}, u32[]{:S(2)}) copy-start(f32[8,4096]{1,0:T(8,128)} %decay_ref.3) | copy-start | bytes 393220
  4.0 11.9 %collective-permute-start = (f32[136,256]{1,0:T(8,128)S(1)}, f32[136,256]{1,0:T(8,128)S(1)}, u32[]{:S(2)}, u32[]{:S(2)}) collective-permute-start(f32[136,256]{1,0:T(8,128)S(1)} %get-tuple-element.22), channel_id=1, source_target_pairs={{0,4},{4,8},{1,5},{5,9},{2,6},{6,10},{3,7},{7,11},{16,20},{20,24},... | collective-permute-start | bytes 417800 | tf_op jit(solution)/shard_map/ppermute | solution.py:435
  9.0 7.0 %collective-permute-start.1 = (f32[136,256]{1,0:T(8,128)S(1)}, f32[136,256]{1,0:T(8,128)S(1)}, u32[]{:S(2)}, u32[]{:S(2)}) collective-permute-start(f32[136,256]{1,0:T(8,128)S(1)} %get-tuple-element.23), channel_id=1, source_target_pairs={{8,4},{0,8},{9,5},{1,9},{10,6},{2,10},{11,7},{3,11},{24,20},{16,24... | collective-permute-start | bytes 417800 | tf_op jit(solution)/shard_map/ppermute | solution.py:436
  11.3 8.9 %copy-start = (bf16[4096,512]{1,0:T(8,128)(2,1)S(1)}, bf16[4096,512]{1,0:T(8,128)(2,1)}, u32[]{:S(2)}) copy-start(bf16[4096,512]{1,0:T(8,128)(2,1)} %gate_ref.1) | copy-start | bytes 12582916
  16.0 8.0 %collective-permute-start.2 = (f32[128,256]{1,0:T(8,128)S(1)}, f32[128,256]{1,0:T(8,128)S(1)}, u32[]{:S(2)}, u32[]{:S(2)}) collective-permute-start(f32[128,256]{1,0:T(8,128)S(1)} %get-tuple-element.31), channel_id=1, source_target_pairs={{0,4},{4,8},{8,12},{1,5},{5,9},{9,13},{2,6},{6,10},{10,14},{3,7},{... | collective-permute-start | bytes 393224 | tf_op jit(solution)/shard_map/ppermute | solution.py:441
  19.5 4.5 %copy-start.3 = (f32[512]{0:T(512)S(1)}, f32[512]{0:T(512)}, u32[]{:S(2)}) copy-start(f32[512]{0:T(512)} %param.11) | copy-start | bytes 6148
  19.5 4.4 %collective-permute-start.3 = (f32[128,256]{1,0:T(8,128)S(1)}, f32[128,256]{1,0:T(8,128)S(1)}, u32[]{:S(2)}, u32[]{:S(2)}) collective-permute-start(f32[128,256]{1,0:T(8,128)S(1)} %get-tuple-element.32), channel_id=1, source_target_pairs={{4,12},{5,13},{6,14},{7,15},{20,28},{21,29},{22,30},{23,31}} | collective-permute-start | bytes 393224 | tf_op jit(solution)/shard_map/ppermute | solution.py:442
